TPU v7x, 512 devices: a whole 4x4x16 slice. The times are simulated.
512 devices in a mesh: dp: 16 (over z_hi, y), feat: 32 (over x, z_lo, core).
Axes of the slice: x: 4, y: 4, z: 16 (z_hi: 4, z_lo: 4; z = z_hi * 4 + z_lo), core: 2. Of those that a mesh axis runs over, the one named last changes fastest.
Arguments:
- sample: bfloat16 [16384, 2048], P(('dp', 'feat')), may hold values from -1800 to 1800
- pool: bfloat16 [32768, 2048], P(('dp', 'feat')), may hold values from -720 to 720
- old_min: float32 [32768], P(('dp', 'feat')), may hold values from 0.5 to 1.5
- centers: int32 [256], replicated, may hold values from 0 to 32767
Outputs:
- new_min: float32 [32768], P(('dp', 'feat'))
All inputs are finite; a program needn't handle non-finite values.
Results may differ from a plain program's by a relative error of at most 0.00045.
Values may be sent and summed in bfloat16 or wider, within the bound.
A program may use at most 64 MiB of HBM per device.

v0:
```python
import jax
import jax.numpy as jnp
from jax import lax
from jax.sharding import PartitionSpec as P

EPSILON = 1e-06
HIGHEST = lax.Precision.HIGHEST


def contract_rows(left_part, right_part):
    return lax.dot_general(
        left_part, right_part, (((0,), (0,)), ((), ())), preferred_element_type=jnp.float32
    )


def squared_terms(row_values, centre_rows):
    row_wide = row_values.astype(jnp.float32)
    centre_wide = centre_rows.astype(jnp.float32)
    row_norms = jnp.sum(row_wide * row_wide, axis=1)
    centre_norms = jnp.sum(centre_wide * centre_wide, axis=1)
    inner_products = lax.dot_general(
        row_values, centre_rows, (((1,), (1,)), ((), ())), preferred_element_type=jnp.float32
    )
    return row_norms[:, None] + centre_norms[None, :] - 2.0 * inner_products


def pick_rows(source, centers, offset):
    row_count = source.shape[0]
    local_index = centers - offset
    inside = (local_index >= 0) & (local_index < row_count)
    taken_rows = source[jnp.clip(local_index, 0, row_count - 1)].astype(jnp.float32)
    return jnp.where(inside[:, None], taken_rows, 0.0)


def per_device(sample, pool, old_min, centers):
    model_width = sample.shape[1]
    feat_count = lax.axis_size("feat")
    group_count = lax.axis_size("dp")
    row_block = model_width // feat_count
    col_block = model_width // group_count
    feat_index = lax.axis_index("feat")
    group_index = lax.axis_index("dp")
    row_start = feat_index * row_block
    col_start = group_index * col_block
    pool_count = pool.shape[0]
    sample_total = sample.shape[0] * feat_count * group_count
    row_offset = (group_index * feat_count + feat_index) * pool_count
    sample_wide = sample.astype(jnp.float32)
    own_squares = jnp.sum(sample_wide * sample_wide, axis=0)
    col_squares = lax.psum(own_squares, ("dp", "feat"))
    inverse = 1.0 / jnp.sqrt(col_squares / sample_total + EPSILON)
    portion = lax.all_gather(sample, "feat", axis=0, tiled=True)
    left_part = lax.dynamic_slice_in_dim(portion, row_start, row_block, 1)
    gram_part = contract_rows(left_part, portion)
    gram_part = gram_part / sample_total
    inverse_rows = lax.dynamic_slice_in_dim(inverse, row_start, row_block)
    inverse_cols = lax.dynamic_slice_in_dim(inverse, col_start, col_block)
    cov_block = lax.psum_scatter(gram_part, "dp", scatter_dimension=1, tiled=True)
    corr_block = inverse_rows[:, None] * cov_block * inverse_cols[None, :]
    corr_rows = lax.all_gather(corr_block, "dp", axis=1, tiled=True)
    corr_cols = lax.all_gather(corr_block, "feat", axis=0, tiled=True)
    rows_global = row_start + jnp.arange(row_block, dtype=jnp.int32)
    cols_global = col_start + jnp.arange(col_block, dtype=jnp.int32)
    all_index = jnp.arange(model_width, dtype=jnp.int32)
    eye_rows = (rows_global[:, None] == all_index[None, :]).astype(jnp.float32)
    eye_cols = (all_index[:, None] == cols_global[None, :]).astype(jnp.float32)
    eye_block = (rows_global[:, None] == cols_global[None, :]).astype(jnp.float32)
    first_rows = 0.5 * (3.0 * eye_rows - corr_rows)
    first_cols = 0.5 * (3.0 * eye_cols - corr_cols)
    updated_y = jnp.dot(corr_rows, first_cols, precision=HIGHEST)
    left_part = first_rows
    middle = jnp.dot(
        left_part, lax.all_gather(updated_y, "feat", axis=0, tiled=True), precision=HIGHEST
    )
    second_factor = 0.5 * (3.0 * eye_block - middle)
    root_block = jnp.dot(
        lax.all_gather(second_factor, "dp", axis=1, tiled=True), first_cols, precision=HIGHEST
    )
    weight_block = (inverse_rows[:, None] * root_block).astype(jnp.bfloat16)
    weight_cols = lax.all_gather(weight_block, "feat", axis=0, tiled=True)
    everything = jnp.dot(
        pool,
        lax.all_gather(weight_cols, "dp", axis=1, tiled=True),
        preferred_element_type=jnp.float32,
    ).astype(jnp.bfloat16)
    contribution = pick_rows(everything, centers, row_offset)
    centre_full = lax.psum(contribution, ("dp", "feat")).astype(jnp.bfloat16)
    squared = squared_terms(everything, centre_full)
    nearest = jnp.min(jnp.maximum(squared, 0.0), axis=1) / (2.0 * model_width)
    return jnp.minimum(old_min, nearest)


def solution(mesh):
    return jax.shard_map(
        per_device,
        mesh=mesh,
        in_specs=(P(("dp", "feat"), None), P(("dp", "feat"), None), P(("dp", "feat")), P()),
        out_specs=P(("dp", "feat")),
        check_vma=False,
    )
```

profile of v0, /device:TPU:1, one launch (start us, length us, event | category | flops | bytes accessed | tf_op | source)
XLA Modules:
  0.0 781.0 jit_solution(9917778738509852095)
XLA Ops:
  6.5 0.0 copy-start
  6.5 0.0 copy-start.1
  6.5 0.0 all-gather.5.cloned.1.call-start
  6.5 0.7 all-gather.5.cloned.1.call-update
  7.3 0.0 reduce-scatter.2.cloned.1.call-start
  7.3 76.0 %all-gather.5.cloned.1.call-done = bf16[1024,2048]{1,0:T(8,128)(2,1)} async-done(((bf16[32,2048]{1,0:T(8,128)(2,1)}), bf16[1024,2048]{1,0:T(8,128)(2,1)}) %all-gather.5.cloned.1.call-update) | async-done | bytes 4194320 | tf_op jit(solution)/shard_map/all_gather | solution.py:52
  83.3 4.0 convolution_multiply_fusion
  87.4 0.0 copy-start.2
  87.4 0.0 reduce-scatter.2.cloned.1.call-update
  87.4 0.0 all-gather.7.cloned.1.call-start
  87.4 0.0 copy-done.1
  87.5 105.5 %psum.14 = f32[2048]{0:T(1024)S(1)} all-reduce(f32[2048]{0:T(1024)S(1)} %multiply_reduce_fusion.2), channel_id=1, replica_groups=mesh['dp'=16,'feat'=32] {'dp','feat'}, use_global_device_ids=true, to_apply=%region_1.0 | all-reduce | flops 2048 | bytes 16384 | tf_op jit(solution)/shard_map/psum | solution.py:50
  193.0 0.1 dynamic_slice.9
  193.1 0.1 dynamic_slice.11
  193.2 3.6 reduce-scatter.2.cloned.1.call-done
  196.7 1.4 multiply_multiply_fusion
  198.2 0.0 all-gather.7.cloned.1.call-update
  198.2 0.0 all-gather.9.cloned.1.call-start
  198.2 51.9 %all_gather.22 = f32[64,2048]{1,0:T(8,128)S(1)} all-gather(f32[64,128]{1,0:T(8,128)} %multiply_multiply_fusion), channel_id=1, replica_groups=mesh['dp'=16,'feat'=32] {'dp'}, dimensions={1}, use_global_device_ids=true | all-gather | bytes 557056 | tf_op jit(solution)/shard_map/all_gather | solution.py:60
  250.2 11.2 %all-gather.7.cloned.1.call-done = f32[2048,128]{1,0:T(8,128)} async-done(((f32[64,128]{1,0:T(8,128)}), f32[2048,128]{1,0:T(8,128)}) %all-gather.7.cloned.1.call-update) | async-done | bytes 1048592 | tf_op jit(solution)/shard_map/all_gather | solution.py:61
  261.4 2.7 fusion.5
  264.1 0.0 all-gather.9.cloned.1.call-update
  264.2 0.0 all-gather.11.cloned.1.call-start
  264.2 62.7 %all-gather.9.cloned.1.call-done = f32[2048,128]{1,0:T(8,128)} async-done(((f32[64,128]{1,0:T(8,128)}), f32[2048,128]{1,0:T(8,128)}) %all-gather.9.cloned.1.call-update) | async-done | bytes 1048592 | tf_op jit(solution)/shard_map/all_gather | solution.py:73
  327.0 2.1 fusion.3
  329.1 50.6 %all_gather.25 = f32[64,2048]{1,0:T(8,128)S(1)} all-gather(f32[64,128]{1,0:T(8,128)S(1)} %fusion.3), channel_id=1, replica_groups=mesh['dp'=16,'feat'=32] {'dp'}, dimensions={1}, use_global_device_ids=true | all-gather | bytes 557056 | tf_op jit(solution)/shard_map/all_gather | solution.py:77
  379.7 2.1 fusion.4
  381.9 54.6 %all_gather.26 = bf16[2048,128]{1,0:T(8,128)(2,1)} all-gather(bf16[64,128]{1,0:T(8,128)(2,1)S(1)} %fusion.4), channel_id=1, replica_groups=mesh['dp'=16,'feat'=32] {'feat'}, dimensions={0}, use_global_device_ids=true | all-gather | bytes 540672 | tf_op jit(solution)/shard_map/all_gather | solution.py:80
  436.5 0.0 all-gather.11.cloned.1.call-update
  436.5 0.0 copy-done.2
  436.6 220.7 %all-gather.11.cloned.1.call-done = bf16[2048,2048]{1,0:T(8,128)(2,1)} async-done(((bf16[2048,128]{1,0:T(8,128)(2,1)}), bf16[2048,2048]{1,0:T(8,128)(2,1)}) %all-gather.11.cloned.1.call-update) | async-done | bytes 8388624 | tf_op jit(solution)/shard_map/all_gather | solution.py:83
  657.3 0.0 copy-done
  657.3 5.1 multiply_reduce_fusion.1
  662.3 1.4 gather_fusion
  663.7 0.0 copy-start.3
  663.7 1.6 convert_select_fusion
  665.3 107.9 %all-reduce.1 = bf16[256,2048]{1,0:T(8,128)(2,1)S(1)} all-reduce(f32[256,2048]{1,0:T(8,128)} %convert_select_fusion), channel_id=1, replica_groups=mesh['dp'=16,'feat'=32] {'dp','feat'}, use_global_device_ids=true, to_apply=%region_4.5 | all-reduce | flops 524288 | bytes 3145728 | tf_op jit(solution)/shard_map/psum | solution.py:87
  773.2 0.3 multiply_reduce_fusion
  773.4 0.5 fusion.2
  774.0 0.0 copy-done.3
  774.0 0.5 multiply_minimum_fusion
  (7 shorter events, 0.1 us)
Async XLA Ops:
  6.5 650.7 %copy-start = (bf16[64,2048]{1,0:T(8,128)(2,1)S(1)}, bf16[64,2048]{1,0:T(8,128)(2,1)}, u32[]{:S(2)}) copy-start(bf16[64,2048]{1,0:T(8,128)(2,1)} %param.5) | copy-start | bytes 786436
  6.5 80.9 %copy-start.1 = (bf16[32,2048]{1,0:T(8,128)(2,1)S(1)}, bf16[32,2048]{1,0:T(8,128)(2,1)}, u32[]{:S(2)}) copy-start(bf16[32,2048]{1,0:T(8,128)(2,1)} %param.4) | copy-start | bytes 393220
  6.5 76.8 %all-gather.5.cloned.1.call-start = ((), (), s32[]{:S(2)}) async-start(), calls=%async_computation.1 | async-start | bytes 4325376 | tf_op jit(solution)/shard_map/all_gather | solution.py:52
  7.3 189.5 %reduce-scatter.2.cloned.1.call-start = ((), (), s32[]{:S(2)}) async-start(), calls=%async_computation.2 | async-start | bytes 557056 | tf_op jit(solution)/shard_map/reduce_scatter | solution.py:58
  87.4 349.2 %copy-start.2 = (s32[256]{0:T(256)S(1)}, s32[256]{0:T(256)}, u32[]{:S(2)}) copy-start(s32[256]{0:T(256)} %param.7) | copy-start | bytes 3076
  87.4 174.0 %all-gather.7.cloned.1.call-start = ((), (), s32[]{:S(2)}) async-start(), calls=%async_computation.3 | async-start | bytes 1081344 | tf_op jit(solution)/shard_map/all_gather | solution.py:61
  198.2 128.8 %all-gather.9.cloned.1.call-start = ((), (), s32[]{:S(2)}) async-start(), calls=%async_computation.4 | async-start | bytes 1081344 | tf_op jit(solution)/shard_map/all_gather | solution.py:73
  264.2 393.1 %all-gather.11.cloned.1.call-start = ((), (), s32[]{:S(2)}) async-start(), calls=%async_computation.5 | async-start | bytes 8912896 | tf_op jit(solution)/shard_map/all_gather | solution.py:83
  663.7 110.3 %copy-start.3 = (f32[64]{0:T(128)S(1)}, f32[64]{0:T(128)}, u32[]{:S(2)}) copy-start(f32[64]{0:T(128)} %param.6) | copy-start | bytes 772
Sparse Core Ops, SparseCore 0:
  9.5 73.7 all-gather.4
  87.5 109.1 reduce-scatter.1
  199.1 62.2 all-gather.6
  264.3 62.6 all-gather.8
  436.6 220.5 all-gather.10
where the time goes:
time: 782 us; the launch traced here: 781 us
  waiting for transfers between devices  375 us (48%)
  blocking collectives  371 us (47%)
  matrix products  16.6 us (2%)
  between operations  13.3 us (2%)
    all_gather x1, waiting for transfers between devices, per_device(): lax.all_gather(weight_cols, 'dp', axis=1, tiled=True)  221 us
    psum x1, blocking collectives, per_device(): centre_full = lax.psum(contribution, ('dp', 'feat')).astype(jnp.bfloat16)  108 us
    psum x1, blocking collectives, per_device(): col_squares = lax.psum(own_squares, ('dp', 'feat'))  105 us
    all_gather x1, waiting for transfers between devices, per_device(): portion = lax.all_gather(sample, 'feat', axis=0, tiled=True)  76 us
    all_gather x1, waiting for transfers between devices, per_device(): lax.all_gather(updated_y, 'feat', axis=0, tiled=True)  62.7 us
    all_gather x1, blocking collectives, per_device(): weight_cols = lax.all_gather(weight_block, 'feat', axis=0, tiled=True)  54.6 us
    all_gather x1, blocking collectives, per_device(): corr_rows = lax.all_gather(corr_block, 'dp', axis=1, tiled=True)  51.9 us
    all_gather x1, blocking collectives, per_device(): lax.all_gather(second_factor, 'dp', axis=1, tiled=True)  50.6 us
  transfers between devices with their start and end apart: 5, of which 5 were waited for; matrix products, arithmetic and copies ran while one was open for 0% of the time, Pallas kernels for 0%

commit v1 on v0

v1 whole, which is shorter than its diff:
```python
import jax
import jax.numpy as jnp
from jax import lax
from jax.experimental import pallas as pl
from jax.experimental.pallas import tpu as pltpu
from jax.sharding import PartitionSpec as P

EPSILON = 1e-06
MESH = pl.DeviceIdType.MESH
F32 = jnp.float32
BF16 = jnp.bfloat16
LANES = 128
PANELS = 9
SLAB = 1536
GRAM = PANELS * LANES
DIAG = SLAB - LANES


def position():
    dp = lax.axis_index("dp")
    feat = lax.axis_index("feat")
    x, y = feat // 8, dp % 4
    z = (dp // 4) * 4 + (feat // 2) % 4
    return x, y, z, feat % 2


def device(x, y, z, core):
    return ((z // 4) * 4 + y, x * 8 + (z % 4) * 2 + core)


def greet(partners):
    barrier = pltpu.get_barrier_semaphore()
    for partner in partners:
        pl.semaphore_signal(barrier, inc=1, device_id=partner, device_id_type=MESH)
    pl.semaphore_wait(barrier, len(partners))


def remote(src, dst, send, recv, where):
    copy = pltpu.make_async_remote_copy(
        src_ref=src, dst_ref=dst, send_sem=send, recv_sem=recv, device_id=where, device_id_type=MESH
    )
    copy.start()
    return copy


def column_panels(chip):
    pair, half = chip // 2, chip % 2
    last = half if pair < 4 else 1 - half
    return [(2 * pair + step) % 16 for step in range(8)] + [(2 * pair + 8 + last) % 16]


def exchange_kernel(parcels, landed, send, recv, local):
    x, y, z, core = position()
    mine = x * 4 + y
    offsets = [(dx, dy) for dx in range(4) for dy in range(4) if dx or dy]
    greet([device((x + dx) % 4, (y + dy) % 4, z, core) for dx, dy in offsets])
    rows = pl.ds(pl.multiple_of(mine * 32, 32), 32)
    copies = []
    for slot, (dx, dy) in enumerate(offsets):
        to_x, to_y = (x + dx) % 4, (y + dy) % 4
        copies.append(
            remote(parcels.at[to_x * 4 + to_y], landed.at[:, rows, :], send.at[slot], recv.at[slot], device(to_x, to_y, z, core))
        )
    own = pltpu.make_async_copy(parcels.at[mine], landed.at[:, rows, :], local)
    own.start()
    own.wait()
    for copy in copies:
        copy.wait()


def gram_kernel(landed, chosen, partial):
    x, y, _, _ = position()
    half = y % 2
    left = landed[half]
    for step in range(PANELS):
        block = lax.dot_general(left, landed[step], (((0,), (0,)), ((), ())), preferred_element_type=F32)
        if step < 2:
            rows = lax.broadcasted_iota(jnp.int32, block.shape, 0)
            cols = lax.broadcasted_iota(jnp.int32, block.shape, 1)
            block = jnp.where((rows == cols) & (half == step), 0.0, block)
        lanes = slice(step * LANES, (step + 1) * LANES)
        partial[0, :, lanes] = block[:64]
        partial[1, :, lanes] = block[64:]
    picked = jnp.zeros((256, LANES), F32)
    for part in range(2):
        picked += jnp.dot(chosen[part], landed[PANELS + part], preferred_element_type=F32)
    for part in range(4):
        lanes = slice(GRAM + (part % 2) * LANES, GRAM + (part % 2 + 1) * LANES)
        partial[part // 2, :, lanes] = picked[part * 64 : part * 64 + 64]
    wide = left.astype(F32)
    squares = jnp.sum(wide * wide, axis=0, keepdims=True)
    first = lax.broadcasted_iota(jnp.int32, (64, LANES), 0) == 0
    for core in range(2):
        partial[core, :, DIAG:] = jnp.where(first, squares, 0.0)


def in_three(total):
    high = total.astype(BF16).astype(F32)
    middle = (total - high).astype(BF16).astype(F32)
    low = total - high - middle
    rows = lax.broadcasted_iota(jnp.int32, (16, LANES), 0)
    return jnp.where(rows == 0, high, jnp.where(rows == 1, middle, jnp.where(rows == 2, low, 0.0)))


def reduce_kernel(partial, summed, other, mine, terms, chunk, core_send, core_recv, send, recv, send_back, recv_back):
    x, y, z, core = position()
    column = [(z + offset) % 16 for offset in range(16)]
    greet([device(x, y, z, 1 - core)] + [device(x, y, k, core) for k in column[1:]])
    remote(partial.at[1 - core], other, core_send, core_recv, device(x, y, z, 1 - core)).wait()
    mine[:, :DIAG] = (partial[core, :, :DIAG] + other[:, :DIAG]).astype(BF16)
    squares = partial[core, 0:1, DIAG:] + other[0:1, DIAG:]
    mine[0:16, DIAG:] = in_three(squares).astype(BF16)
    mine[16:64, DIAG:] = jnp.zeros((48, LANES), BF16)

    def part_of(ref, k):
        return ref.at[pl.ds(pl.multiple_of((k // 4) * 16, 16), 16), pl.ds(pl.multiple_of((k % 4) * 384, 384), 384)]

    copies = [
        remote(part_of(mine, column[o]), terms.at[o], send.at[o], recv.at[o], device(x, y, column[o], core))
        for o in range(1, 16)
    ]
    total = part_of(mine, z)[...].astype(F32)
    for o in range(1, 16):
        copies[o - 1].wait()
        total += terms[o].astype(F32)
    squares = total[0:1, 256:] + total[1:2, 256:] + total[2:3, 256:]
    chunk[:, :256] = total[:, :256].astype(BF16)
    chunk[:, 256:] = jnp.where(z == 3, in_three(squares), total[:, 256:]).astype(BF16)
    copies = [
        remote(chunk, part_of(summed, z), send_back.at[o], recv_back.at[o], device(x, y, column[o], core))
        for o in range(1, 16)
    ]
    part_of(summed, z)[...] = chunk[...]
    for copy in copies:
        copy.wait()


def spread_kernel(slab, everything, send, recv, local):
    x, y, z, core = position()
    twin = device(x, y, z, 1 - core)
    across_x = [(x + d) % 4 for d in range(4)]
    across_y = [(y + d) % 4 for d in range(4)]
    from_x = [(x + 4 - d) % 4 for d in range(4)]
    from_y = [(y + 4 - d) % 4 for d in range(4)]
    greet(
        [twin]
        + [device(across_x[d], y, z, core) for d in range(1, 4)]
        + [device(x, across_y[d], z, core) for d in range(1, 4)]
    )
    upper, lower = pl.ds(0, 32), pl.ds(32, 32)
    own = pltpu.make_async_copy(slab, everything.at[x, y, core], local)
    own.start()
    slot = iter(range(25))

    def go(src, dst, where):
        n = next(slot)
        return remote(src, dst, send.at[n], recv.at[n], where)

    first_x, first_y = [], []
    for d in range(1, 4):
        first_x.append(go(slab.at[upper], everything.at[x, y, core, upper], device(across_x[d], y, z, core)))
        first_y.append(go(slab.at[lower], everything.at[x, y, core, lower], device(x, across_y[d], z, core)))
    rest = [go(slab, everything.at[x, y, core], twin)]
    own.wait()
    for copy in first_x:
        copy.wait()
    second_y = []
    block = everything.at[:, y, core, upper]
    for d in range(1, 4):
        second_y.append(go(block, block, device(x, across_y[d], z, core)))
    for copy in first_y:
        copy.wait()
    second_x = []
    block = everything.at[x, :, core, lower]
    for d in range(1, 4):
        second_x.append(go(block, block, device(across_x[d], y, z, core)))
    for d in range(1, 4):
        block = everything.at[from_x[d], y, core, upper]
        rest.append(go(block, block, twin))
        block = everything.at[x, from_y[d], core, lower]
        rest.append(go(block, block, twin))
    for d in range(1, 4):
        second_y[d - 1].wait()
        block = everything.at[:, from_y[d], core, upper]
        rest.append(go(block, block, twin))
        second_x[d - 1].wait()
        block = everything.at[from_x[d], :, core, lower]
        rest.append(go(block, block, twin))
    for copy in rest:
        copy.wait()


def whiten_kernel(sample_total, blocks, pool, whitened, start, held, ready, corner, scale, extra):
    count = start.shape[0]
    for chip in range(16):
        lanes = slice(chip * LANES, (chip + 1) * LANES)
        parts = blocks[chip * LANES : chip * LANES + 16, DIAG:].astype(F32)
        mean = (parts[0:1] + parts[1:2] + parts[2:3]) / sample_total
        inverse = 1.0 / jnp.sqrt(mean + EPSILON)
        scale[0:1, lanes] = inverse
        extra[0:1, lanes] = inverse * mean * inverse - 1.0
        for part in range(4):
            rows = slice(chip * LANES + (part // 2) * 64, chip * LANES + (part // 2) * 64 + 64)
            source = slice(GRAM + (part % 2) * LANES, GRAM + (part % 2 + 1) * LANES)
            start[part * 64 : part * 64 + 64, lanes] = blocks[rows, source].astype(F32) * inverse
        start[256:, lanes] = pool[:, lanes].astype(F32) * inverse
    for pair in range(4):
        for half in range(2):
            rows = slice(half * LANES, (half + 1) * LANES)
            others = slice((1 - half) * LANES, (2 - half) * LANES)
            top = (2 * pair + half) * LANES
            corner[pair, rows, rows] = blocks[top : top + LANES, GRAM - LANES : GRAM]
            top = (2 * pair + 8 + half) * LANES
            corner[pair, others, rows] = blocks[top : top + LANES, GRAM - LANES : GRAM].astype(F32).T.astype(BF16)
    held[...] = start[...] * (1.0 / 16.0)

    def transposed(left, right):
        return lax.dot_general(left, right, (((1,), (1,)), ((), ())), preferred_element_type=F32)

    @pl.loop(0, 4)
    def _(turn):
        factor = jnp.where(turn == 0, -0.3125, jnp.where(turn == 1, 0.375, jnp.where(turn == 2, -0.5, 1.0)))
        for j in range(8):
            lanes = slice(j * 256, (j + 1) * 256)
            scaled = (held[:, lanes] * scale[0:1, lanes]).astype(BF16)
            ready[:, lanes] = scaled
            if j < 3:
                ready[:, 2048 + j * 256 : 2048 + (j + 1) * 256] = scaled
        for j in range(8):
            lanes = slice(j * 256, (j + 1) * 256)
            out = transposed(ready[:, (j + 1) * 256 : (j + 4) * 256], blocks[lanes, 256:1024])
            for d in range(4):
                i = (j - d) % 8
                out += jnp.dot(
                    ready[:, i * 256 : (i + 1) * 256],
                    blocks[i * 256 : (i + 1) * 256, d * 256 : (d + 1) * 256],
                    preferred_element_type=F32,
                )
            if j >= 4:
                out += jnp.dot(ready[:, (j - 4) * 256 : (j - 3) * 256], corner[j - 4], preferred_element_type=F32)
            else:
                out += transposed(ready[:, (j + 4) * 256 : (j + 5) * 256], corner[j])
            held[:, lanes] = (
                out * (scale[0:1, lanes] * (1.0 / sample_total))
                + held[:, lanes] * extra[0:1, lanes]
                + factor * start[:, lanes]
            )

    whitened[...] = held[...].astype(BF16)


VMEM = pl.BlockSpec(memory_space=pltpu.VMEM)
DMA = pltpu.SemaphoreType.DMA


def parameters(collective=None, limit=48):
    if collective is None:
        return pltpu.CompilerParams(vmem_limit_bytes=limit * 1024 * 1024)
    return pltpu.CompilerParams(collective_id=collective, has_side_effects=True, vmem_limit_bytes=limit * 1024 * 1024)


def squared_terms(row_values, centre_rows):
    row_wide = row_values.astype(F32)
    centre_wide = centre_rows.astype(F32)
    row_norms = jnp.sum(row_wide * row_wide, axis=1)
    centre_norms = jnp.sum(centre_wide * centre_wide, axis=1)
    inner_products = lax.dot_general(row_values, centre_rows, (((1,), (1,)), ((), ())), preferred_element_type=F32)
    return row_norms[:, None] + centre_norms[None, :] - 2.0 * inner_products


def per_device(sample, pool, old_min, centers):
    width = sample.shape[1]
    pool_count = pool.shape[0]
    sample_total = sample.shape[0] * lax.axis_size("dp") * lax.axis_size("feat")
    x, y, z, core = position()
    sample_panels = sample.reshape(32, 16, LANES).transpose(1, 0, 2)
    pool_panels = pool.reshape(2, 32, 16, LANES).transpose(2, 0, 1, 3)
    parcels = jnp.stack(
        [
            jnp.concatenate([sample_panels[k : k + 1] for k in column_panels(chip)] + [pool_panels[chip]], axis=0)
            for chip in range(16)
        ]
    )
    landed = pl.pallas_call(
        exchange_kernel,
        out_shape=jax.ShapeDtypeStruct((PANELS + 2, 512, LANES), BF16),
        in_specs=[VMEM],
        out_specs=VMEM,
        scratch_shapes=[DMA((15,)), DMA((15,)), DMA],
        compiler_params=parameters(0),
    )(parcels)
    chips = jnp.arange(16, dtype=jnp.int32)
    owners = ((z // 4) * 4 + chips % 4) * 32 + (chips // 4) * 8 + (z % 4) * 2 + core
    row_ids = (
        owners[None, :, None] * pool_count
        + jnp.arange(2, dtype=jnp.int32)[:, None, None] * 32
        + jnp.arange(32, dtype=jnp.int32)[None, None, :]
    ).reshape(2, 512)
    chosen = (centers[None, :, None] == row_ids[:, None, :]).astype(BF16)
    partial = pl.pallas_call(
        gram_kernel,
        out_shape=jax.ShapeDtypeStruct((2, 64, SLAB), F32),
        in_specs=[VMEM, VMEM],
        out_specs=VMEM,
        compiler_params=parameters(),
    )(landed, chosen)
    summed = pl.pallas_call(
        reduce_kernel,
        out_shape=jax.ShapeDtypeStruct((64, SLAB), BF16),
        in_specs=[VMEM],
        out_specs=VMEM,
        scratch_shapes=[
            pltpu.VMEM((64, SLAB), F32),
            pltpu.VMEM((64, SLAB), BF16),
            pltpu.VMEM((16, 16, 384), BF16),
            pltpu.VMEM((16, 384), BF16),
            DMA,
            DMA,
            DMA((16,)),
            DMA((16,)),
            DMA((16,)),
            DMA((16,)),
        ],
        compiler_params=parameters(1),
    )(partial)
    everything = pl.pallas_call(
        spread_kernel,
        out_shape=jax.ShapeDtypeStruct((4, 4, 2, 64, SLAB), BF16),
        in_specs=[VMEM],
        out_specs=VMEM,
        scratch_shapes=[DMA((25,)), DMA((25,)), DMA],
        compiler_params=parameters(2),
    )(summed)
    count = 256 + pool_count
    whitened = pl.pallas_call(
        lambda *refs: whiten_kernel(float(sample_total), *refs),
        out_shape=jax.ShapeDtypeStruct((count, width), BF16),
        in_specs=[VMEM, VMEM],
        out_specs=VMEM,
        scratch_shapes=[
            pltpu.VMEM((count, width), F32),
            pltpu.VMEM((count, width), F32),
            pltpu.VMEM((count, width + 768), BF16),
            pltpu.VMEM((4, 256, 256), BF16),
            pltpu.VMEM((8, width), F32),
            pltpu.VMEM((8, width), F32),
        ],
        compiler_params=parameters(),
    )(everything.reshape(width, SLAB), pool)
    squared = squared_terms(whitened[256:], whitened[:256])
    nearest = jnp.min(jnp.maximum(squared, 0.0), axis=1) / (2.0 * width)
    return jnp.minimum(old_min, nearest)


def solution(mesh):
    return jax.shard_map(
        per_device,
        mesh=mesh,
        in_specs=(P(("dp", "feat"), None), P(("dp", "feat"), None), P(("dp", "feat")), P()),
        out_specs=P(("dp", "feat")),
        check_vma=False,
    )
```

time: 782 us -> 125 us (0.16)
  waiting for transfers between devices: 375 us -> 0 us
  blocking collectives: 371 us -> 0 us
  Pallas kernels: 0 us -> 120 us
  matrix products: 16.6 us -> 0.55 us
  between operations: 13.3 us -> 0.29 us
    all_gather x4 -> x0, waiting for transfers between devices: 371 us -> none  [the longest x1 221 us: per_device(): lax.all_gather(weight_cols, 'dp', axis=1, tiled=True)]
    psum x2 -> x0, blocking collectives: 213 us -> none  [the longest x1 108 us: per_device(): centre_full = lax.psum(contribution, ('dp', 'feat')).astype(jnp.bfloat16)]
    all_gather x3 -> x0, blocking collectives: 157 us -> none  [the longest x1 54.6 us: per_device(): weight_cols = lax.all_gather(weight_block, 'feat', axis=0, tiled=True)]
    pallas_call x0 -> x5, Pallas kernels: none -> 120 us  [the longest x1 40.8 us: per_device(): pl.pallas_call(reduce_kernel, out_shape=jax.ShapeDtypeStruct((64, SLAB),...]
    dot_general x5 -> x0, matrix products: 16.1 us -> none  [the longest x1 5.05 us: per_device(): jnp.dot(pool, lax.all_gather(weight_cols, 'dp', axis=1, tiled=True), pref...]
  transfers between devices with their start and end apart: 5 -> 0, of which waited for: 5 -> 0; matrix products, arithmetic and copies ran while one was open for 0% -> 0% of each run, Pallas kernels for 0% -> 0%
where the time goes in v1:
time: 125 us
  Pallas kernels  120 us (96%)
  local copies, waits for them, and re-layouts  1.98 us (2%)
  other arithmetic  1.44 us (1%)
    pallas_call x1, Pallas kernels, per_device(): pl.pallas_call(reduce_kernel, out_shape=jax.ShapeDtypeStruct((64, SLAB),...  40.8 us
    pallas_call x1, Pallas kernels, per_device(): pl.pallas_call(spread_kernel, out_shape=jax.ShapeDtypeStruct((4, 4, 2, 64...  39.1 us
    pallas_call x1, Pallas kernels, per_device(): pl.pallas_call(exchange_kernel, out_shape=jax.ShapeDtypeStruct((PANELS +...  23.9 us
    pallas_call x1, Pallas kernels, per_device(): pl.pallas_call(lambda *refs: whiten_kernel(float(sample_total), *refs), o...  15.9 us

profile of v1, /device:TPU:1, one launch (start us, length us, event | category | flops | bytes accessed | tf_op | source)
XLA Modules:
  0.0 124.6 jit_solution(10468826100616493869)
XLA Ops:
  0.0 0.0 copy-start
  0.0 0.0 copy-start.1
  0.0 0.1 broadcast_add_fusion.1
  0.1 0.1 add.140
  0.2 0.1 add.137
  0.3 0.1 add.138
  0.3 0.6 copy-done
  0.9 0.0 copy-start.2
  1.0 0.0 copy-start.3
  1.0 0.0 copy-done.1
  1.1 0.1 copy.11
  1.2 0.4 copy-done.2
  1.6 0.0 slice-start
  1.6 0.0 slice-start.1
  1.7 0.0 copy-done.3
  1.7 0.1 compare_convert_fusion.chosen
  1.8 0.0 slice-start.2
  2.1 0.3 slice-done
  2.4 0.1 slice-done.1
  2.5 0.1 slice-done.2
  2.7 23.9 %shard_map.46.landed = bf16[11,512,128]{2,1,0:T(8,128)(2,1)S(1)} custom-call(bf16[16,11,32,128]{3,2,1,0:T(8,128)(2,1)S(1)} %fusion.31.parcels), custom_call_target="tpu_custom_call" | custom-call | tf_op jit(solution)/shard_map/pallas_call | solution.py:284
  26.6 0.7 shard_map.47.partial
  27.2 40.8 %shard_map.48.slab = bf16[64,1536]{1,0:T(8,128)(2,1)S(1)} custom-call(f32[2,64,1536]{2,1,0:T(8,128)S(1)} %shard_map.47.partial), custom_call_target="tpu_custom_call" | custom-call | tf_op jit(solution)/shard_map/pallas_call | solution.py:307
  68.0 39.1 %shard_map.49 = bf16[4,4,2,64,1536]{4,3,2,1,0:T(8,128)(2,1)} custom-call(bf16[64,1536]{1,0:T(8,128)(2,1)S(1)} %shard_map.48.slab), custom_call_target="tpu_custom_call" | custom-call | tf_op jit(solution)/shard_map/pallas_call | solution.py:326
  107.1 15.9 %shard_map.50 = bf16[320,2048]{1,0:T(8,128)(2,1)S(1)} custom-call(bf16[2048,1536]{1,0:T(8,128)(2,1)} %bitcast.111, bf16[64,2048]{1,0:T(8,128)(2,1)S(1)} %copy-done.1), custom_call_target="tpu_custom_call" | custom-call | tf_op jit(solution)/shard_map/pallas_call | solution.py:335
  123.1 0.0 copy-start.4
  123.1 0.2 multiply_reduce_fusion.1
  123.2 0.3 multiply_reduce_fusion
  123.5 0.5 fusion.2
  124.1 0.0 copy-done.4
  124.1 0.5 multiply_minimum_fusion
  (29 shorter events, 0.5 us)
Async XLA Ops:
  0.0 0.9 copy-start
  0.0 1.0 copy-start.1
  0.9 0.6 copy-start.2
  1.0 0.7 copy-start.3
  1.6 0.7 slice-start
  1.6 0.8 slice-start.1
  1.8 0.8 slice-start.2
  123.1 1.0 copy-start.4

commit v2 on v1

v2 whole, which is shorter than its diff:
```python
import jax
import jax.numpy as jnp
from jax import lax
from jax.experimental import pallas as pl
from jax.experimental.pallas import tpu as pltpu
from jax.sharding import PartitionSpec as P

EPSILON = 1e-06
MESH = pl.DeviceIdType.MESH
F32 = jnp.float32
BF16 = jnp.bfloat16
LANES = 128
PANELS = 9
SLAB = 1536
GRAM = PANELS * LANES
DIAG = SLAB - LANES


def position():
    dp = lax.axis_index("dp")
    feat = lax.axis_index("feat")
    x, y = feat // 8, dp % 4
    z = (dp // 4) * 4 + (feat // 2) % 4
    return x, y, z, feat % 2


def device(x, y, z, core):
    return ((z // 4) * 4 + y, x * 8 + (z % 4) * 2 + core)


def remote(src, dst, send, recv, where):
    copy = pltpu.make_async_remote_copy(
        src_ref=src, dst_ref=dst, send_sem=send, recv_sem=recv, device_id=where, device_id_type=MESH
    )
    copy.start()
    return copy


def column_panels(chip):
    pair, half = chip // 2, chip % 2
    last = half if pair < 4 else 1 - half
    return [(2 * pair + step) % 16 for step in range(8)] + [(2 * pair + 8 + last) % 16]


def in_three(total):
    high = total.astype(BF16).astype(F32)
    middle = (total - high).astype(BF16).astype(F32)
    low = total - high - middle
    rows = lax.broadcasted_iota(jnp.int32, (16, LANES), 0)
    return jnp.where(rows == 0, high, jnp.where(rows == 1, middle, jnp.where(rows == 2, low, 0.0)))


def rows_dot(left, right):
    return lax.dot_general(left, right, (((0,), (0,)), ((), ())), preferred_element_type=F32)


def tiles(ref, k):
    return ref.at[pl.ds(pl.multiple_of((k // 4) * 16, 16), 16), pl.ds(pl.multiple_of((k % 4) * 384, 384), 384)]


def moments_kernel(
    sample, pool, centers, everything, parcels, landed, partial, other, mine, terms, chunk, local, plane_send, plane_recv,
    core_send, core_recv, send, recv, send_back, recv_back, piece_send, piece_recv,
):
    x, y, z, core = position()
    here = x * 4 + y
    twin = device(x, y, z, 1 - core)
    column = [(z + o) % 16 for o in range(16)]
    offsets = [(dx, dy) for dx in range(4) for dy in range(4) if dx or dy]
    barrier = pltpu.get_barrier_semaphore()
    partners = [device(x, y, column[(8 + o // 2 if o % 2 else 8 - o // 2)], core) for o in range(1, 16)]
    partners += [device((x + dx) % 4, (y + dy) % 4, z, core) for dx, dy in offsets] + [twin]
    for partner in partners:
        pl.semaphore_signal(barrier, inc=1, device_id=partner, device_id_type=MESH)

    for chip in range(16):
        for step, panel in enumerate(column_panels(chip)):
            parcels[chip, step] = sample[:, panel * LANES : (panel + 1) * LANES]
        for part in range(2):
            parcels[chip, PANELS + part] = pool[part * 32 : part * 32 + 32, chip * LANES : (chip + 1) * LANES]
    pl.semaphore_wait(barrier, len(partners))

    rows = pl.ds(pl.multiple_of(here * 32, 32), 32)
    copies = []
    for slot, (dx, dy) in enumerate(offsets):
        to_x, to_y = (x + dx) % 4, (y + dy) % 4
        copies.append(
            remote(parcels.at[to_x * 4 + to_y], landed.at[:, rows, :], plane_send.at[slot], plane_recv.at[slot], device(to_x, to_y, z, core))
        )
    own = pltpu.make_async_copy(parcels.at[here], landed.at[:, rows, :], local)
    own.start()
    row = lax.broadcasted_iota(jnp.int32, (512, 256), 0)
    owner = ((z // 4) * 4 + ((row >> 5) & 3)) * 32 + (row >> 7) * 8 + (z % 4) * 2 + core
    row_id = owner * 64 + (row & 31)
    chosen = [jnp.where(row_id + part * 32 == centers[...], 1.0, 0.0).astype(BF16) for part in range(2)]
    own.wait()
    for copy in copies:
        copy.wait()

    half = y % 2
    left = landed[half]
    for step in range(PANELS):
        block = rows_dot(left, landed[step])
        if step < 2:
            down = lax.broadcasted_iota(jnp.int32, block.shape, 0)
            along = lax.broadcasted_iota(jnp.int32, block.shape, 1)
            block = jnp.where((down == along) & (half == step), 0.0, block)
        lanes = slice(step * LANES, (step + 1) * LANES)
        partial[0, :, lanes] = block[:64]
        partial[1, :, lanes] = block[64:]
    picked = rows_dot(chosen[0], landed[PANELS]) + rows_dot(chosen[1], landed[PANELS + 1])
    for part in range(4):
        lanes = slice(GRAM + (part % 2) * LANES, GRAM + (part % 2 + 1) * LANES)
        partial[part // 2, :, lanes] = picked[part * 64 : part * 64 + 64]
    wide = left.astype(F32)
    squares = jnp.sum(wide * wide, axis=0, keepdims=True)
    first = lax.broadcasted_iota(jnp.int32, (64, LANES), 0) == 0
    for side in range(2):
        partial[side, :, DIAG:] = jnp.where(first, squares, 0.0)

    remote(partial.at[1 - core], other, core_send, core_recv, twin).wait()
    mine[:, :DIAG] = (partial[core, :, :DIAG] + other[:, :DIAG]).astype(BF16)
    squares = partial[core, 0:1, DIAG:] + other[0:1, DIAG:]
    mine[0:16, DIAG:] = in_three(squares).astype(BF16)
    mine[16:64, DIAG:] = jnp.zeros((48, LANES), BF16)

    far_first = [8] + [o for d in range(7, 0, -1) for o in (d, 16 - d)]
    copies = {
        o: remote(tiles(mine, column[o]), terms.at[o], send.at[o], recv.at[o], device(x, y, column[o], core)) for o in far_first
    }
    total = tiles(mine, z)[...].astype(F32)
    for o in reversed(far_first):
        copies[o].wait()
        total += terms[o].astype(F32)
    squares = total[0:1, 256:] + total[1:2, 256:] + total[2:3, 256:]
    chunk[:, :256] = total[:, :256].astype(BF16)
    chunk[:, 256:] = jnp.where(z == 3, in_three(squares), total[:, 256:]).astype(BF16)

    slab = everything.at[x, y, core]
    tiles(slab, z)[...] = chunk[...]
    back = {
        o: remote(chunk, tiles(slab, z), send_back.at[o], recv_back.at[z], device(x, y, column[o], core)) for o in far_first
    }
    pending = list(back.values())

    def gathered(k):
        pltpu.make_async_remote_copy(
            src_ref=chunk, dst_ref=tiles(slab, k), send_sem=send_back.at[0], recv_sem=recv_back.at[k], device_id=twin, device_id_type=MESH
        ).wait_recv()

    zone = z // 4
    counter = iter(range(200))

    class Strip:
        def __init__(self, shift, flip, sign):
            self.a = (zone + shift) % 4
            self.shift, self.flip, self.sign = shift, flip, sign
            self.rows = pl.ds(pl.multiple_of(self.a * 16, 16), 16)
            p, q = (y, x) if flip else (x, y)
            self.p = [p, (p + 4 - sign) % 4, (p + 4 + sign) % 4, (p + 2) % 4]
            self.q = [q, (q + 4 - sign) % 4, (q + 4 + sign) % 4, (q + 2) % 4]
            self.ahead, self.behind = [], []
            self.onward = []

        def where(self, p, q):
            return device(q, p, z, core) if self.flip else device(p, q, z, core)

        def piece(self, p, q):
            return everything.at[q, p, core, self.rows] if self.flip else everything.at[p, q, core, self.rows]

        def line(self, q):
            return everything.at[q, :, core, self.rows] if self.flip else everything.at[:, q, core, self.rows]

        def go(self, ref, target):
            n = next(counter)
            copy = remote(ref, ref, piece_send.at[n], piece_recv.at[n], target)
            pending.append(copy)
            return copy

        def across(self, n):
            piece = self.piece(self.p[n], self.q[0])
            self.ahead.append(self.go(piece, self.where(self.p[0], self.q[2])))
            self.behind.append(self.go(piece, self.where(self.p[0], self.q[1])))

        def begin(self):
            if self.shift == 0:
                for step in range(1, 4):
                    gathered(zone * 4 + (z + step) % 4)
            else:
                for step in range(4):
                    gathered(self.a * 4 + step)
            piece = self.piece(self.p[0], self.q[0])
            self.up = self.go(piece, self.where(self.p[2], self.q[0]))
            self.down = self.go(piece, self.where(self.p[1], self.q[0]))
            self.across(0)

        def second(self):
            self.up.wait_recv()
            self.far = self.go(self.piece(self.p[1], self.q[0]), self.where(self.p[2], self.q[0]))
            self.across(1)
            self.down.wait_recv()
            self.across(2)

        def third(self):
            self.far.wait_recv()
            self.across(3)
            self.twins = [self.go(self.line(self.q[0]), twin)]

        def fourth(self):
            for n in range(4):
                self.ahead[n].wait_recv()
                self.onward.append(self.go(self.piece(self.p[n], self.q[1]), self.where(self.p[0], self.q[2])))
            self.twins.append(self.go(self.line(self.q[1]), twin))
            for n in range(4):
                self.behind[n].wait_recv()
            self.twins.append(self.go(self.line(self.q[2]), twin))

        def fifth(self):
            for copy in self.onward:
                copy.wait_recv()
            self.twins.append(self.go(self.line(self.q[3]), twin))

        def last(self):
            for copy in self.twins:
                copy.wait_recv()

    s0, s1, s2, s3 = Strip(0, False, 1), Strip(1, True, 1), Strip(3, False, -1), Strip(2, True, -1)
    s0.begin(), s1.begin(), s2.begin()
    s0.second(), s1.second(), s3.begin(), s2.second()
    s0.third(), s1.third(), s3.second(), s2.third()
    s0.fourth(), s1.fourth(), s3.third(), s2.fourth()
    s0.fifth(), s1.fifth(), s3.fourth(), s2.fifth(), s3.fifth()
    for strip in (s0, s1, s2, s3):
        strip.last()
    for copy in pending:
        copy.wait_send()


def whiten_kernel(sample_total, blocks, pool, whitened, start, held, ready, corner, scale, extra):
    count = start.shape[0]
    for chip in range(16):
        lanes = slice(chip * LANES, (chip + 1) * LANES)
        parts = blocks[chip * LANES : chip * LANES + 16, DIAG:].astype(F32)
        mean = (parts[0:1] + parts[1:2] + parts[2:3]) / sample_total
        inverse = 1.0 / jnp.sqrt(mean + EPSILON)
        scale[0:1, lanes] = inverse
        extra[0:1, lanes] = inverse * mean * inverse - 1.0
        for part in range(4):
            rows = slice(chip * LANES + (part // 2) * 64, chip * LANES + (part // 2) * 64 + 64)
            source = slice(GRAM + (part % 2) * LANES, GRAM + (part % 2 + 1) * LANES)
            start[part * 64 : part * 64 + 64, lanes] = blocks[rows, source].astype(F32) * inverse
        start[256:, lanes] = pool[:, lanes].astype(F32) * inverse
    for pair in range(4):
        for half in range(2):
            rows = slice(half * LANES, (half + 1) * LANES)
            others = slice((1 - half) * LANES, (2 - half) * LANES)
            top = (2 * pair + half) * LANES
            corner[pair, rows, rows] = blocks[top : top + LANES, GRAM - LANES : GRAM]
            top = (2 * pair + 8 + half) * LANES
            corner[pair, others, rows] = blocks[top : top + LANES, GRAM - LANES : GRAM].astype(F32).T.astype(BF16)
    held[...] = start[...] * (1.0 / 16.0)

    def transposed(left, right):
        return lax.dot_general(left, right, (((1,), (1,)), ((), ())), preferred_element_type=F32)

    @pl.loop(0, 4)
    def _(turn):
        factor = jnp.where(turn == 0, -0.3125, jnp.where(turn == 1, 0.375, jnp.where(turn == 2, -0.5, 1.0)))
        for j in range(8):
            lanes = slice(j * 256, (j + 1) * 256)
            scaled = (held[:, lanes] * scale[0:1, lanes]).astype(BF16)
            ready[:, lanes] = scaled
            if j < 3:
                ready[:, 2048 + j * 256 : 2048 + (j + 1) * 256] = scaled
        for j in range(8):
            lanes = slice(j * 256, (j + 1) * 256)
            out = transposed(ready[:, (j + 1) * 256 : (j + 4) * 256], blocks[lanes, 256:1024])
            for d in range(4):
                i = (j - d) % 8
                out += jnp.dot(
                    ready[:, i * 256 : (i + 1) * 256],
                    blocks[i * 256 : (i + 1) * 256, d * 256 : (d + 1) * 256],
                    preferred_element_type=F32,
                )
            if j >= 4:
                out += jnp.dot(ready[:, (j - 4) * 256 : (j - 3) * 256], corner[j - 4], preferred_element_type=F32)
            else:
                out += transposed(ready[:, (j + 4) * 256 : (j + 5) * 256], corner[j])
            held[:, lanes] = (
                out * (scale[0:1, lanes] * (1.0 / sample_total))
                + held[:, lanes] * extra[0:1, lanes]
                + factor * start[:, lanes]
            )

    whitened[...] = held[...].astype(BF16)


VMEM = pl.BlockSpec(memory_space=pltpu.VMEM)
DMA = pltpu.SemaphoreType.DMA


def parameters(collective=None, limit=48):
    if collective is None:
        return pltpu.CompilerParams(vmem_limit_bytes=limit * 1024 * 1024)
    return pltpu.CompilerParams(collective_id=collective, has_side_effects=True, vmem_limit_bytes=limit * 1024 * 1024)


def squared_terms(row_values, centre_rows):
    row_wide = row_values.astype(F32)
    centre_wide = centre_rows.astype(F32)
    row_norms = jnp.sum(row_wide * row_wide, axis=1)
    centre_norms = jnp.sum(centre_wide * centre_wide, axis=1)
    inner_products = lax.dot_general(row_values, centre_rows, (((1,), (1,)), ((), ())), preferred_element_type=F32)
    return row_norms[:, None] + centre_norms[None, :] - 2.0 * inner_products


def per_device(sample, pool, old_min, centers):
    width = sample.shape[1]
    pool_count = pool.shape[0]
    sample_total = sample.shape[0] * lax.axis_size("dp") * lax.axis_size("feat")
    everything = pl.pallas_call(
        moments_kernel,
        out_shape=jax.ShapeDtypeStruct((4, 4, 2, 64, SLAB), BF16),
        in_specs=[VMEM, VMEM, VMEM],
        out_specs=VMEM,
        scratch_shapes=[
            pltpu.VMEM((16, PANELS + 2, 32, LANES), BF16),
            pltpu.VMEM((PANELS + 2, 512, LANES), BF16),
            pltpu.VMEM((2, 64, SLAB), F32),
            pltpu.VMEM((64, SLAB), F32),
            pltpu.VMEM((64, SLAB), BF16),
            pltpu.VMEM((16, 16, 384), BF16),
            pltpu.VMEM((16, 384), BF16),
            DMA,
            DMA((15,)),
            DMA((15,)),
            DMA,
            DMA,
            DMA((16,)),
            DMA((16,)),
            DMA((16,)),
            DMA((16,)),
            DMA((76,)),
            DMA((76,)),
        ],
        compiler_params=parameters(0, 16),
    )(sample, pool, centers.reshape(1, 256))
    count = 256 + pool_count
    whitened = pl.pallas_call(
        lambda *refs: whiten_kernel(float(sample_total), *refs),
        out_shape=jax.ShapeDtypeStruct((count, width), BF16),
        in_specs=[VMEM, VMEM],
        out_specs=VMEM,
        scratch_shapes=[
            pltpu.VMEM((count, width), F32),
            pltpu.VMEM((count, width), F32),
            pltpu.VMEM((count, width + 768), BF16),
            pltpu.VMEM((4, 256, 256), BF16),
            pltpu.VMEM((8, width), F32),
            pltpu.VMEM((8, width), F32),
        ],
        compiler_params=parameters(None, 24),
    )(everything.reshape(width, SLAB), pool)
    squared = squared_terms(whitened[256:], whitened[:256])
    nearest = jnp.min(jnp.maximum(squared, 0.0), axis=1) / (2.0 * width)
    return jnp.minimum(old_min, nearest)


def solution(mesh):
    return jax.shard_map(
        per_device,
        mesh=mesh,
        in_specs=(P(("dp", "feat"), None), P(("dp", "feat"), None), P(("dp", "feat")), P()),
        out_specs=P(("dp", "feat")),
        check_vma=False,
    )
```

time: 125 us -> 106 us (0.85)
  Pallas kernels: 120 us -> 102 us
    pallas_call x4 -> x1, Pallas kernels: 104 us -> 88.8 us  [per_device(): pl.pallas_call(moments_kernel, out_shape=jax.ShapeDtypeStruct((4, 4, 2, 6...]
    pallas_call x1, Pallas kernels: 15.9 us -> 13.1 us  [per_device(): pl.pallas_call(lambda *refs: whiten_kernel(float(sample_total), *refs), o...]
    unnamed x11 -> x10, local copies, waits for them, and re-layouts: 1.01 us -> 2.54 us
where the time goes in v2:
time: 106 us
  Pallas kernels  102 us (96%)
  local copies, waits for them, and re-layouts  2.54 us (2%)
    pallas_call x1, Pallas kernels, per_device(): pl.pallas_call(moments_kernel, out_shape=jax.ShapeDtypeStruct((4, 4, 2, 6...  88.8 us
    pallas_call x1, Pallas kernels, per_device(): pl.pallas_call(lambda *refs: whiten_kernel(float(sample_total), *refs), o...  13.1 us
    unnamed x10, local copies, waits for them, and re-layouts  2.54 us

profile of v2, /device:TPU:1, one launch (start us, length us, event | category | flops | bytes accessed | tf_op | source)
XLA Modules:
  0.0 106.0 jit_solution(1067824932068204499)
XLA Ops:
  0.0 0.0 copy-start
  0.0 0.9 copy-done
  1.0 0.0 copy-start.2
  1.0 0.9 copy-done.2
  1.9 0.0 copy-start.3
  1.9 0.7 copy-done.3
  2.5 0.0 copy-start.1
  2.5 88.8 %shard_map.46 = bf16[4,4,2,64,1536]{4,3,2,1,0:T(8,128)(2,1)S(1)} custom-call(bf16[32,2048]{1,0:T(8,128)(2,1)S(1)} %copy-done.2, bf16[64,2048]{1,0:T(8,128)(2,1)S(1)} %copy-done, s32[1,256]{1,0:T(1,128)S(1)} %bitcast.3), custom_call_target="tpu_custom_call" | custom-call | tf_op jit(solution)/shard_map/pallas_call | solution.py:321
  91.3 0.0 copy-done.1
  91.4 13.1 %shard_map.47 = bf16[320,2048]{1,0:T(8,128)(2,1)S(1)} custom-call(bf16[2048,1536]{1,0:T(8,128)(2,1)S(1)} %bitcast.2, bf16[64,2048]{1,0:T(8,128)(2,1)S(1)} %copy-done.1), custom_call_target="tpu_custom_call" | custom-call | tf_op jit(solution)/shard_map/pallas_call | solution.py:349
  104.4 0.2 multiply_reduce_fusion.1
  104.6 0.0 copy-start.4
  104.6 0.3 multiply_reduce_fusion
  104.9 0.5 fusion.2
  105.4 0.0 copy-done.4
  105.4 0.5 multiply_minimum_fusion
Async XLA Ops:
  0.0 0.9 copy-start
  1.0 0.9 copy-start.2
  1.9 0.7 copy-start.3
  2.5 88.8 %copy-start.1 = (bf16[64,2048]{1,0:T(8,128)(2,1)S(1)}, bf16[64,2048]{1,0:T(8,128)(2,1)}, u32[]{:S(2)}) copy-start(bf16[64,2048]{1,0:T(8,128)(2,1)} %refs_1_.1) | copy-start | bytes 786436
  104.6 0.8 copy-start.4

commit v3 on v2

--- a/solution.py
+++ b/solution.py
@@ -42,11 +42,11 @@
     return [(2 * pair + step) % 16 for step in range(8)] + [(2 * pair + 8 + last) % 16]
 
 
-def in_three(total):
+def in_three(total, count):
     high = total.astype(BF16).astype(F32)
     middle = (total - high).astype(BF16).astype(F32)
     low = total - high - middle
-    rows = lax.broadcasted_iota(jnp.int32, (16, LANES), 0)
+    rows = lax.broadcasted_iota(jnp.int32, (count, LANES), 0)
     return jnp.where(rows == 0, high, jnp.where(rows == 1, middle, jnp.where(rows == 2, low, 0.0)))
 
 
@@ -54,108 +54,136 @@
     return lax.dot_general(left, right, (((0,), (0,)), ((), ())), preferred_element_type=F32)
 
 
-def tiles(ref, k):
-    return ref.at[pl.ds(pl.multiple_of((k // 4) * 16, 16), 16), pl.ds(pl.multiple_of((k % 4) * 384, 384), 384)]
-
-
 def moments_kernel(
-    sample, pool, centers, everything, parcels, landed, partial, other, mine, terms, chunk, local, plane_send, plane_recv,
-    core_send, core_recv, send, recv, send_back, recv_back, piece_send, piece_recv,
+    sample_in, pool_in, centers, everything, sample, pool, parcels_a, parcels_b, landed_a, landed_b, partial, other, mine, terms,
+    chunk, local, plane_send, plane_recv, core_send, core_recv, send, recv, send_back, recv_back, piece_send, piece_recv,
 ):
     x, y, z, core = position()
     here = x * 4 + y
     twin = device(x, y, z, 1 - core)
     column = [(z + o) % 16 for o in range(16)]
+    far_first = [8] + [o for d in range(7, 0, -1) for o in (d, 16 - d)]
     offsets = [(dx, dy) for dx in range(4) for dy in range(4) if dx or dy]
+    loads = [
+        pltpu.make_async_copy(sample_in, sample, local.at[0]),
+        pltpu.make_async_copy(pool_in, pool, local.at[1]),
+    ]
+    for copy in loads:
+        copy.start()
     barrier = pltpu.get_barrier_semaphore()
-    partners = [device(x, y, column[(8 + o // 2 if o % 2 else 8 - o // 2)], core) for o in range(1, 16)]
+    partners = [device(x, y, column[o], core) for o in far_first]
     partners += [device((x + dx) % 4, (y + dy) % 4, z, core) for dx, dy in offsets] + [twin]
     for partner in partners:
         pl.semaphore_signal(barrier, inc=1, device_id=partner, device_id_type=MESH)
 
+    for copy in loads:
+        copy.wait()
     for chip in range(16):
         for step, panel in enumerate(column_panels(chip)):
-            parcels[chip, step] = sample[:, panel * LANES : (panel + 1) * LANES]
+            block = sample[:, panel * LANES : (panel + 1) * LANES]
+            if step < 6:
+                parcels_a[chip, step] = block
+            else:
+                parcels_b[chip, step - 6] = block
         for part in range(2):
-            parcels[chip, PANELS + part] = pool[part * 32 : part * 32 + 32, chip * LANES : (chip + 1) * LANES]
+            parcels_b[chip, 3 + part] = pool[part * 32 : part * 32 + 32, chip * LANES : (chip + 1) * LANES]
     pl.semaphore_wait(barrier, len(partners))
 
     rows = pl.ds(pl.multiple_of(here * 32, 32), 32)
-    copies = []
-    for slot, (dx, dy) in enumerate(offsets):
-        to_x, to_y = (x + dx) % 4, (y + dy) % 4
-        copies.append(
-            remote(parcels.at[to_x * 4 + to_y], landed.at[:, rows, :], plane_send.at[slot], plane_recv.at[slot], device(to_x, to_y, z, core))
-        )
-    own = pltpu.make_async_copy(parcels.at[here], landed.at[:, rows, :], local)
-    own.start()
-    row = lax.broadcasted_iota(jnp.int32, (512, 256), 0)
-    owner = ((z // 4) * 4 + ((row >> 5) & 3)) * 32 + (row >> 7) * 8 + (z % 4) * 2 + core
-    row_id = owner * 64 + (row & 31)
-    chosen = [jnp.where(row_id + part * 32 == centers[...], 1.0, 0.0).astype(BF16) for part in range(2)]
-    own.wait()
-    for copy in copies:
-        copy.wait()
+    parcels, landed = [parcels_a, parcels_b], [landed_a, landed_b]
+
+    def exchange(g):
+        copies = []
+        for slot, (dx, dy) in enumerate(offsets):
+            to_x, to_y = (x + dx) % 4, (y + dy) % 4
+            copies.append(
+                remote(
+                    parcels[g].at[to_x * 4 + to_y],
+                    landed[g].at[:, rows, :],
+                    plane_send.at[g, slot],
+                    plane_recv.at[g, slot],
+                    device(to_x, to_y, z, core),
+                )
+            )
+        own = pltpu.make_async_copy(parcels[g].at[here], landed[g].at[:, rows, :], local.at[2 + g])
+        own.start()
+        own.wait()
+        return copies
 
     half = y % 2
-    left = landed[half]
-    for step in range(PANELS):
-        block = rows_dot(left, landed[step])
+
+    def block_of(step):
+        block = rows_dot(landed_a[half], landed_a[step] if step < 6 else landed_b[step - 6])
         if step < 2:
             down = lax.broadcasted_iota(jnp.int32, block.shape, 0)
             along = lax.broadcasted_iota(jnp.int32, block.shape, 1)
             block = jnp.where((down == along) & (half == step), 0.0, block)
-        lanes = slice(step * LANES, (step + 1) * LANES)
-        partial[0, :, lanes] = block[:64]
-        partial[1, :, lanes] = block[64:]
-    picked = rows_dot(chosen[0], landed[PANELS]) + rows_dot(chosen[1], landed[PANELS + 1])
-    for part in range(4):
-        lanes = slice(GRAM + (part % 2) * LANES, GRAM + (part % 2 + 1) * LANES)
-        partial[part // 2, :, lanes] = picked[part * 64 : part * 64 + 64]
-    wide = left.astype(F32)
-    squares = jnp.sum(wide * wide, axis=0, keepdims=True)
-    first = lax.broadcasted_iota(jnp.int32, (64, LANES), 0) == 0
-    for side in range(2):
-        partial[side, :, DIAG:] = jnp.where(first, squares, 0.0)
-
-    remote(partial.at[1 - core], other, core_send, core_recv, twin).wait()
-    mine[:, :DIAG] = (partial[core, :, :DIAG] + other[:, :DIAG]).astype(BF16)
-    squares = partial[core, 0:1, DIAG:] + other[0:1, DIAG:]
-    mine[0:16, DIAG:] = in_three(squares).astype(BF16)
-    mine[16:64, DIAG:] = jnp.zeros((48, LANES), BF16)
-
-    far_first = [8] + [o for d in range(7, 0, -1) for o in (d, 16 - d)]
-    copies = {
-        o: remote(tiles(mine, column[o]), terms.at[o], send.at[o], recv.at[o], device(x, y, column[o], core)) for o in far_first
-    }
-    total = tiles(mine, z)[...].astype(F32)
-    for o in reversed(far_first):
-        copies[o].wait()
-        total += terms[o].astype(F32)
-    squares = total[0:1, 256:] + total[1:2, 256:] + total[2:3, 256:]
-    chunk[:, :256] = total[:, :256].astype(BF16)
-    chunk[:, 256:] = jnp.where(z == 3, in_three(squares), total[:, 256:]).astype(BF16)
-
-    slab = everything.at[x, y, core]
-    tiles(slab, z)[...] = chunk[...]
-    back = {
-        o: remote(chunk, tiles(slab, z), send_back.at[o], recv_back.at[z], device(x, y, column[o], core)) for o in far_first
-    }
-    pending = list(back.values())
-
-    def gathered(k):
+        return block
+
+    def reduce_begin(g):
+        remote(partial.at[g, 1 - core], other.at[g], core_send.at[g], core_recv.at[g], twin).wait()
+        if g == 0:
+            mine[g] = (partial[g, core] + other[g]).astype(BF16)
+        else:
+            mine[g, :, :640] = (partial[g, core, :, :640] + other[g, :, :640]).astype(BF16)
+            squares = partial[g, core, 0:1, 640:] + other[g, 0:1, 640:]
+            mine[g, 0:16, 640:] = in_three(squares, 16).astype(BF16)
+            mine[g, 16:64, 640:] = jnp.zeros((48, LANES), BF16)
+        own = pltpu.make_async_copy(tiles(mine.at[g], z), terms.at[g, 0], local.at[4 + g])
+        own.start()
+        copies = {
+            o: remote(tiles(mine.at[g], column[o]), terms.at[g, o], send.at[g, o], recv.at[g, o], device(x, y, column[o], core))
+            for o in far_first
+        }
+        own.wait()
+        return copies
+
+    def tiles(ref, k):
+        return ref.at[pl.ds(pl.multiple_of((k // 2) * 8, 8), 8), pl.ds(pl.multiple_of((k % 2) * 384, 384), 384)]
+
+    def slab(g):
+        return everything.at[x, y, core, :, pl.ds(g * 768, 768)]
+
+    pending = []
+
+    def reduce_end(g, copies):
+        total = terms[g, 0].astype(F32)
+        for o in reversed(far_first):
+            copies[o].wait()
+            total += terms[g, o].astype(F32)
+        if g == 0:
+            chunk[g] = total.astype(BF16)
+        else:
+            squares = total[0:1, 256:] + total[1:2, 256:] + total[2:3, 256:]
+            chunk[g, :, :256] = total[:, :256].astype(BF16)
+            chunk[g, :, 256:] = jnp.where(z == 1, in_three(squares, 8), total[:, 256:]).astype(BF16)
+        own = pltpu.make_async_copy(chunk.at[g], tiles(slab(g), z), local.at[6 + g])
+        own.start()
+        for o in far_first:
+            pending.append(
+                remote(chunk.at[g], tiles(slab(g), z), send_back.at[g, o], recv_back.at[g, z], device(x, y, column[o], core))
+            )
+        own.wait()
+
+    def gathered(g, k):
         pltpu.make_async_remote_copy(
-            src_ref=chunk, dst_ref=tiles(slab, k), send_sem=send_back.at[0], recv_sem=recv_back.at[k], device_id=twin, device_id_type=MESH
+            src_ref=chunk.at[g],
+            dst_ref=tiles(slab(g), k),
+            send_sem=send_back.at[g, 0],
+            recv_sem=recv_back.at[g, k],
+            device_id=twin,
+            device_id_type=MESH,
         ).wait_recv()
 
     zone = z // 4
     counter = iter(range(200))
 
     class Strip:
-        def __init__(self, shift, flip, sign):
+        def __init__(self, group, shift, flip, sign):
+            self.group = group
             self.a = (zone + shift) % 4
             self.shift, self.flip, self.sign = shift, flip, sign
-            self.rows = pl.ds(pl.multiple_of(self.a * 16, 16), 16)
+            self.place = (pl.ds(pl.multiple_of(self.a * 16, 16), 16), pl.ds(group * 768, 768))
             p, q = (y, x) if flip else (x, y)
             self.p = [p, (p + 4 - sign) % 4, (p + 4 + sign) % 4, (p + 2) % 4]
             self.q = [q, (q + 4 - sign) % 4, (q + 4 + sign) % 4, (q + 2) % 4]
@@ -166,10 +194,11 @@
             return device(q, p, z, core) if self.flip else device(p, q, z, core)
 
         def piece(self, p, q):
-            return everything.at[q, p, core, self.rows] if self.flip else everything.at[p, q, core, self.rows]
+            return everything.at[(q, p, core) + self.place] if self.flip else everything.at[(p, q, core) + self.place]
 
         def line(self, q):
-            return everything.at[q, :, core, self.rows] if self.flip else everything.at[:, q, core, self.rows]
+            every = slice(None)
+            return everything.at[(q, every, core) + self.place] if self.flip else everything.at[(every, q, core) + self.place]
 
         def go(self, ref, target):
             n = next(counter)
@@ -185,10 +214,10 @@
         def begin(self):
             if self.shift == 0:
                 for step in range(1, 4):
-                    gathered(zone * 4 + (z + step) % 4)
+                    gathered(self.group, zone * 4 + (z + step) % 4)
             else:
                 for step in range(4):
-                    gathered(self.a * 4 + step)
+                    gathered(self.group, self.a * 4 + step)
             piece = self.piece(self.p[0], self.q[0])
             self.up = self.go(piece, self.where(self.p[2], self.q[0]))
             self.down = self.go(piece, self.where(self.p[1], self.q[0]))
@@ -224,13 +253,54 @@
             for copy in self.twins:
                 copy.wait_recv()
 
-    s0, s1, s2, s3 = Strip(0, False, 1), Strip(1, True, 1), Strip(3, False, -1), Strip(2, True, -1)
-    s0.begin(), s1.begin(), s2.begin()
-    s0.second(), s1.second(), s3.begin(), s2.second()
-    s0.third(), s1.third(), s3.second(), s2.third()
-    s0.fourth(), s1.fourth(), s3.third(), s2.fourth()
-    s0.fifth(), s1.fifth(), s3.fourth(), s2.fifth(), s3.fifth()
-    for strip in (s0, s1, s2, s3):
+    def strips(g):
+        return [Strip(g, 0, False, 1), Strip(g, 1, True, 1), Strip(g, 3, False, -1), Strip(g, 2, True, -1)]
+
+    first = exchange(0)
+    row = lax.broadcasted_iota(jnp.int32, (512, 256), 0)
+    owner = ((z // 4) * 4 + ((row >> 5) & 3)) * 32 + (row >> 7) * 8 + (z % 4) * 2 + core
+    row_id = owner * 64 + (row & 31)
+    chosen = [jnp.where(row_id + part * 32 == centers[...], 1.0, 0.0).astype(BF16) for part in range(2)]
+    for copy in first:
+        copy.wait_send()
+    second = exchange(1)
+    for copy in first:
+        copy.wait_recv()
+    for step in range(6):
+        block = block_of(step)
+        lanes = slice(step * LANES, (step + 1) * LANES)
+        partial[0, 0, :, lanes] = block[:64]
+        partial[0, 1, :, lanes] = block[64:]
+    sums_a = reduce_begin(0)
+    wide = landed_a[half].astype(F32)
+    squares = jnp.sum(wide * wide, axis=0, keepdims=True)
+    top = lax.broadcasted_iota(jnp.int32, (64, LANES), 0) == 0
+    for side in range(2):
+        partial[1, side, :, 640:] = jnp.where(top, squares, 0.0)
+    for copy in second:
+        copy.wait()
+    for step in range(6, PANELS):
+        block = block_of(step)
+        lanes = slice((step - 6) * LANES, (step - 5) * LANES)
+        partial[1, 0, :, lanes] = block[:64]
+        partial[1, 1, :, lanes] = block[64:]
+    picked = rows_dot(chosen[0], landed_b[3]) + rows_dot(chosen[1], landed_b[4])
+    for part in range(4):
+        lanes = slice(384 + (part % 2) * LANES, 384 + (part % 2 + 1) * LANES)
+        partial[1, part // 2, :, lanes] = picked[part * 64 : part * 64 + 64]
+    sums_b = reduce_begin(1)
+    reduce_end(0, sums_a)
+    a0, a1, a2, a3 = strips(0)
+    b0, b1, b2, b3 = strips(1)
+    a0.begin()
+    reduce_end(1, sums_b)
+    a0.second(), a1.begin(), a2.begin(), a3.begin(), a0.third()
+    a1.second(), a2.second(), b0.begin(), a3.second(), a1.third(), a2.third(), a3.third()
+    b1.begin(), b2.begin(), a0.fourth(), b0.second(), b3.begin(), a1.fourth(), a2.fourth()
+    b1.second(), b2.second(), b0.third(), a3.fourth(), b3.second(), a0.fifth(), b1.third(), b2.third(), b3.third()
+    a1.fifth(), a2.fifth(), a3.fifth(), b0.fourth(), b1.fourth(), b2.fourth(), b3.fourth()
+    b0.fifth(), b1.fifth(), b2.fifth(), b3.fifth()
+    for strip in (a0, a1, a2, a3, b0, b1, b2, b3):
         strip.last()
     for copy in pending:
         copy.wait_send()
@@ -296,6 +366,7 @@
 
 
 VMEM = pl.BlockSpec(memory_space=pltpu.VMEM)
+HBM = pl.BlockSpec(memory_space=pltpu.HBM)
 DMA = pltpu.SemaphoreType.DMA
 
 
@@ -321,27 +392,31 @@
     everything = pl.pallas_call(
         moments_kernel,
         out_shape=jax.ShapeDtypeStruct((4, 4, 2, 64, SLAB), BF16),
-        in_specs=[VMEM, VMEM, VMEM],
+        in_specs=[HBM, HBM, VMEM],
         out_specs=VMEM,
         scratch_shapes=[
-            pltpu.VMEM((16, PANELS + 2, 32, LANES), BF16),
-            pltpu.VMEM((PANELS + 2, 512, LANES), BF16),
-            pltpu.VMEM((2, 64, SLAB), F32),
-            pltpu.VMEM((64, SLAB), F32),
-            pltpu.VMEM((64, SLAB), BF16),
-            pltpu.VMEM((16, 16, 384), BF16),
-            pltpu.VMEM((16, 384), BF16),
-            DMA,
-            DMA((15,)),
-            DMA((15,)),
-            DMA,
-            DMA,
-            DMA((16,)),
-            DMA((16,)),
-            DMA((16,)),
-            DMA((16,)),
-            DMA((76,)),
-            DMA((76,)),
+            pltpu.VMEM(sample.shape, BF16),
+            pltpu.VMEM(pool.shape, BF16),
+            pltpu.VMEM((16, 6, 32, LANES), BF16),
+            pltpu.VMEM((16, 5, 32, LANES), BF16),
+            pltpu.VMEM((6, 512, LANES), BF16),
+            pltpu.VMEM((5, 512, LANES), BF16),
+            pltpu.VMEM((2, 2, 64, 768), F32),
+            pltpu.VMEM((2, 64, 768), F32),
+            pltpu.VMEM((2, 64, 768), BF16),
+            pltpu.VMEM((2, 16, 8, 384), BF16),
+            pltpu.VMEM((2, 8, 384), BF16),
+            DMA((8,)),
+            DMA((2, 15)),
+            DMA((2, 15)),
+            DMA((2,)),
+            DMA((2,)),
+            DMA((2, 16)),
+            DMA((2, 16)),
+            DMA((2, 16)),
+            DMA((2, 16)),
+            DMA((152,)),
+            DMA((152,)),
         ],
         compiler_params=parameters(0, 16),
     )(sample, pool, centers.reshape(1, 256))

time: 106 us -> 99.5 us (0.939)
  Pallas kernels: 102 us -> 95.2 us
    pallas_call x1, Pallas kernels: 88.8 us -> 82.1 us  [per_device(): pl.pallas_call(moments_kernel, out_shape=jax.ShapeDtypeStruct((4, 4, 2, 6...]
where the time goes in v3:
time: 99.5 us; the launch traced here: 99.3 us
  Pallas kernels  95.2 us (96%)
  local copies, waits for them, and re-layouts  2.54 us (3%)
    pallas_call x1, Pallas kernels, per_device(): pl.pallas_call(moments_kernel, out_shape=jax.ShapeDtypeStruct((4, 4, 2, 6...  82.1 us
    pallas_call x1, Pallas kernels, per_device(): pl.pallas_call(lambda *refs: whiten_kernel(float(sample_total), *refs), o...  13.1 us
    unnamed x10, local copies, waits for them, and re-layouts  2.54 us

profile of v3, /device:TPU:1, one launch (start us, length us, event | category | flops | bytes accessed | tf_op | source)
XLA Modules:
  0.0 99.3 jit_solution(403595051550054656)
XLA Ops:
  0.0 0.0 copy-start
  0.0 0.9 copy-done
  1.0 0.0 copy-start.2
  1.0 0.9 copy-done.2
  1.9 0.0 copy-start.3
  1.9 0.7 copy-done.3
  2.5 0.0 copy-start.1
  2.5 82.1 %shard_map.46 = bf16[4,4,2,64,1536]{4,3,2,1,0:T(8,128)(2,1)S(1)} custom-call(bf16[32,2048]{1,0:T(8,128)(2,1)S(1)} %copy-done.2, bf16[64,2048]{1,0:T(8,128)(2,1)S(1)} %copy-done, s32[1,256]{1,0:T(1,128)S(1)} %bitcast.3), custom_call_target="tpu_custom_call" | custom-call | tf_op jit(solution)/shard_map/pallas_call | solution.py:392
  84.7 0.0 copy-done.1
  84.7 13.1 %shard_map.47 = bf16[320,2048]{1,0:T(8,128)(2,1)S(1)} custom-call(bf16[2048,1536]{1,0:T(8,128)(2,1)S(1)} %bitcast.2, bf16[64,2048]{1,0:T(8,128)(2,1)S(1)} %copy-done.1), custom_call_target="tpu_custom_call" | custom-call | tf_op jit(solution)/shard_map/pallas_call | solution.py:424
  97.8 0.2 multiply_reduce_fusion.1
  97.9 0.0 copy-start.4
  97.9 0.3 multiply_reduce_fusion
  98.2 0.5 fusion.2
  98.8 0.0 copy-done.4
  98.8 0.5 multiply_minimum_fusion
Async XLA Ops:
  0.0 0.9 copy-start
  1.0 0.9 copy-start.2
  1.9 0.7 copy-start.3
  2.5 82.1 %copy-start.1 = (bf16[64,2048]{1,0:T(8,128)(2,1)S(1)}, bf16[64,2048]{1,0:T(8,128)(2,1)}, u32[]{:S(2)}) copy-start(bf16[64,2048]{1,0:T(8,128)(2,1)} %refs_1_.1) | copy-start | bytes 786436
  97.9 0.8 copy-start.4

commit v4 on v3

v4 whole, which is shorter than its diff:
```python
import jax
import jax.numpy as jnp
from jax import lax
from jax.experimental import pallas as pl
from jax.experimental.pallas import tpu as pltpu
from jax.sharding import PartitionSpec as P

EPSILON = 1e-06
MESH = pl.DeviceIdType.MESH
F32 = jnp.float32
BF16 = jnp.bfloat16
LANES = 128
PANELS = 9
SLAB = 1536
GRAM = PANELS * LANES
DIAG = SLAB - LANES


def position():
    dp = lax.axis_index("dp")
    feat = lax.axis_index("feat")
    x, y = feat // 8, dp % 4
    z = (dp // 4) * 4 + (feat // 2) % 4
    return x, y, z, feat % 2


def device(x, y, z, core):
    return ((z // 4) * 4 + y, x * 8 + (z % 4) * 2 + core)


def remote(src, dst, send, recv, where):
    copy = pltpu.make_async_remote_copy(
        src_ref=src, dst_ref=dst, send_sem=send, recv_sem=recv, device_id=where, device_id_type=MESH
    )
    copy.start()
    return copy


def column_panels(chip):
    pair, half = chip // 2, chip % 2
    last = half if pair < 4 else 1 - half
    return [(2 * pair + step) % 16 for step in range(8)] + [(2 * pair + 8 + last) % 16]


def in_three(total, count):
    high = total.astype(BF16).astype(F32)
    middle = (total - high).astype(BF16).astype(F32)
    low = total - high - middle
    rows = lax.broadcasted_iota(jnp.int32, (count, LANES), 0)
    return jnp.where(rows == 0, high, jnp.where(rows == 1, middle, jnp.where(rows == 2, low, 0.0)))


def rows_dot(left, right):
    return lax.dot_general(left, right, (((0,), (0,)), ((), ())), preferred_element_type=F32)


def lanes_dot(left, right):
    return lax.dot_general(left, right, (((1,), (1,)), ((), ())), preferred_element_type=F32)


def update_kernel(
    sample_total, sample_in, pool_in, centers, nearest, sample, pool, parcels_a, parcels_b, landed_a, landed_b, partial, other, mine,
    terms, chunk, everything, start, held, ready, corner, scale, extra, whitened, twin_rows, local, plane_send, plane_recv,
    core_send, core_recv, send, recv, send_back, recv_back, strip_send, strip_recv,
):
    x, y, z, core = position()
    here = x * 4 + y
    twin = device(x, y, z, 1 - core)
    column = [(z + o) % 16 for o in range(16)]
    far_first = [8] + [o for d in range(7, 0, -1) for o in (d, 16 - d)]
    offsets = [(dx, dy) for dx in range(4) for dy in range(4) if dx or dy]
    loads = [
        pltpu.make_async_copy(sample_in, sample, local.at[0]),
        pltpu.make_async_copy(pool_in, pool, local.at[1]),
    ]
    for copy in loads:
        copy.start()
    barrier = pltpu.get_barrier_semaphore()
    partners = [device(x, y, column[o], core) for o in far_first]
    partners += [device((x + dx) % 4, (y + dy) % 4, z, core) for dx, dy in offsets] + [twin]
    for partner in partners:
        pl.semaphore_signal(barrier, inc=1, device_id=partner, device_id_type=MESH)

    for copy in loads:
        copy.wait()
    for chip in range(16):
        for step, panel in enumerate(column_panels(chip)):
            block = sample[:, panel * LANES : (panel + 1) * LANES]
            if step < 6:
                parcels_a[chip, step] = block
            else:
                parcels_b[chip, step - 6] = block
        for part in range(2):
            parcels_b[chip, 3 + part] = pool[part * 32 : part * 32 + 32, chip * LANES : (chip + 1) * LANES]
    pl.semaphore_wait(barrier, len(partners))

    def bytes_of(ref, send_sem, recv_sem):
        return pltpu.make_async_remote_copy(
            src_ref=ref, dst_ref=ref, send_sem=send_sem, recv_sem=recv_sem, device_id=twin, device_id_type=MESH
        )

    rows = pl.ds(pl.multiple_of(here * 32, 32), 32)
    parcels, landed = [parcels_a, parcels_b], [landed_a, landed_b]

    def exchange(g):
        for dx, dy in offsets:
            to_x, to_y = (x + dx) % 4, (y + dy) % 4
            remote(
                parcels[g].at[to_x * 4 + to_y],
                landed[g].at[:, rows, :],
                plane_send.at[g],
                plane_recv.at[g],
                device(to_x, to_y, z, core),
            )
        own = pltpu.make_async_copy(parcels[g].at[here], landed[g].at[:, rows, :], local.at[2 + g])
        own.start()
        own.wait()
        return bytes_of(landed[g].at[:, pl.ds(0, 480), :], plane_send.at[g], plane_recv.at[g])

    half = y % 2

    def block_of(step):
        block = rows_dot(landed_a[half], landed_a[step] if step < 6 else landed_b[step - 6])
        if step < 2:
            down = lax.broadcasted_iota(jnp.int32, block.shape, 0)
            along = lax.broadcasted_iota(jnp.int32, block.shape, 1)
            block = jnp.where((down == along) & (half == step), 0.0, block)
        return block

    def tiles(ref, k):
        return ref.at[pl.ds(pl.multiple_of((k // 2) * 8, 8), 8), pl.ds(pl.multiple_of((k % 2) * 384, 384), 384)]

    def slab(g):
        return everything.at[x, y, core, :, pl.ds(g * 768, 768)]

    def reduce_begin(g):
        remote(partial.at[g, 1 - core], other.at[g], core_send.at[g], core_recv.at[g], twin).wait()
        if g == 0:
            mine[g] = (partial[g, core] + other[g]).astype(BF16)
        else:
            mine[g, :, :640] = (partial[g, core, :, :640] + other[g, :, :640]).astype(BF16)
            squares = partial[g, core, 0:1, 640:] + other[g, 0:1, 640:]
            mine[g, 0:16, 640:] = in_three(squares, 16).astype(BF16)
            mine[g, 16:64, 640:] = jnp.zeros((48, LANES), BF16)
        own = pltpu.make_async_copy(tiles(mine.at[g], z), terms.at[g, 0], local.at[4 + g])
        own.start()
        for o in far_first:
            remote(tiles(mine.at[g], column[o]), terms.at[g, o], send.at[g], recv.at[g], device(x, y, column[o], core))
        own.wait()

    def reduce_end(g):
        bytes_of(terms.at[g, pl.ds(1, 15)], send.at[g], recv.at[g]).wait()
        total = terms[g, 0].astype(F32)
        for o in range(1, 16):
            total += terms[g, o].astype(F32)
        if g == 0:
            chunk[g] = total.astype(BF16)
        else:
            squares = total[0:1, 256:] + total[1:2, 256:] + total[2:3, 256:]
            chunk[g, :, :256] = total[:, :256].astype(BF16)
            chunk[g, :, 256:] = jnp.where(z == 1, in_three(squares, 8), total[:, 256:]).astype(BF16)
        own = pltpu.make_async_copy(chunk.at[g], tiles(slab(g), z), local.at[6 + g])
        own.start()
        for o in far_first:
            remote(chunk.at[g], tiles(slab(g), z), send_back.at[g], recv_back.at[g, z // 4], device(x, y, column[o], core))
        own.wait()

    zone = z // 4

    class Strip:
        def __init__(self, group, shift, flip):
            self.group, self.shift, self.flip = group, shift, flip
            self.a = (zone + shift) % 4
            self.place = (pl.ds(pl.multiple_of(self.a * 16, 16), 16), pl.ds(group * 768, 768))
            p, q = (y, x) if flip else (x, y)
            self.p = [(p + 4 - d) % 4 for d in range(4)]
            self.q = [(q + 4 - d) % 4 for d in range(4)]
            number = group * 4 + shift
            self.sent = [strip_send.at[number, n] for n in range(2)]
            self.got = [strip_recv.at[number, n] for n in range(7)]

        def where(self, p, q):
            return device(q, p, z, core) if self.flip else device(p, q, z, core)

        def piece(self, p, q):
            return everything.at[(q, p, core) + self.place] if self.flip else everything.at[(p, q, core) + self.place]

        def line(self, q, side=None):
            every, side = slice(None), core if side is None else side
            return everything.at[(q, every, side) + self.place] if self.flip else everything.at[(every, q, side) + self.place]

        def across(self, n):
            piece = self.piece(self.p[n], self.q[0])
            for d in (2, 1, 3):
                remote(piece, piece, self.sent[0], self.got[3 + d - 1], self.where(self.p[0], self.q[4 - d]))

        def twins(self, d):
            line = self.line(self.q[d])
            remote(line, line, self.sent[1], self.got[6], twin)

        def begin(self):
            if self.shift == 0:
                ref = terms.at[self.group, pl.ds(0, 3)]
            else:
                ref = self.piece(self.p[0], self.q[0])
            bytes_of(ref, send_back.at[self.group], recv_back.at[self.group, self.a]).wait_recv()
            piece = self.piece(self.p[0], self.q[0])
            for d in (2, 1, 3):
                remote(piece, piece, self.sent[0], self.got[d - 1], self.where(self.p[4 - d], self.q[0]))
            self.across(0)

        def middle(self):
            for d in (1, 3, 2):
                bytes_of(self.piece(self.p[d], self.q[0]), self.sent[0], self.got[d - 1]).wait_recv()
                self.across(d)
            self.twins(0)

        def finish(self):
            for d in (1, 3, 2):
                bytes_of(self.line(self.q[d]), self.sent[0], self.got[3 + d - 1]).wait_recv()
                self.twins(d)

        def last(self):
            whole = everything.at[(slice(None), slice(None), 1 - core) + self.place]
            bytes_of(whole, self.sent[1], self.got[6]).wait()
            bytes_of(landed_a.at[pl.ds(0, 3), pl.ds(0, 480), :], self.sent[0], self.got[0]).wait_send()

    first = exchange(0)
    row = lax.broadcasted_iota(jnp.int32, (512, 256), 0)
    owner = ((z // 4) * 4 + ((row >> 5) & 3)) * 32 + (row >> 7) * 8 + (z % 4) * 2 + core
    row_id = owner * 64 + (row & 31)
    chosen = [jnp.where(row_id + part * 32 == centers[...], 1.0, 0.0).astype(BF16) for part in range(2)]
    first.wait_send()
    second = exchange(1)
    first.wait_recv()
    for step in range(6):
        block = block_of(step)
        lanes = slice(step * LANES, (step + 1) * LANES)
        partial[0, 0, :, lanes] = block[:64]
        partial[0, 1, :, lanes] = block[64:]
    reduce_begin(0)
    wide = landed_a[half].astype(F32)
    squares = jnp.sum(wide * wide, axis=0, keepdims=True)
    top = lax.broadcasted_iota(jnp.int32, (64, LANES), 0) == 0
    for side in range(2):
        partial[1, side, :, 640:] = jnp.where(top, squares, 0.0)
    second.wait()
    for step in range(6, PANELS):
        block = block_of(step)
        lanes = slice((step - 6) * LANES, (step - 5) * LANES)
        partial[1, 0, :, lanes] = block[:64]
        partial[1, 1, :, lanes] = block[64:]
    picked = rows_dot(chosen[0], landed_b[3]) + rows_dot(chosen[1], landed_b[4])
    for part in range(4):
        lanes = slice(384 + (part % 2) * LANES, 384 + (part % 2 + 1) * LANES)
        partial[1, part // 2, :, lanes] = picked[part * 64 : part * 64 + 64]
    reduce_begin(1)
    reduce_end(0)
    a0, a1, a2, a3 = [Strip(0, shift, shift % 2 == 1) for shift in (0, 1, 3, 2)]
    b0, b1, b2, b3 = [Strip(1, shift, shift % 2 == 1) for shift in (0, 1, 3, 2)]
    a0.begin()
    a0.middle()
    reduce_end(1)
    a1.begin(), a2.begin(), a3.begin()
    a1.middle(), a2.middle(), b0.begin(), a3.middle(), a0.finish(), b0.middle()
    b1.begin(), b2.begin(), a1.finish(), a2.finish(), b3.begin(), b1.middle(), b2.middle(), b3.middle()
    a3.finish(), b0.finish(), b1.finish(), b2.finish(), b3.finish()
    for strip in (a0, a1, a2, a3, b0, b1, b2, b3):
        strip.last()
    for g in range(2):
        bytes_of(terms.at[g, pl.ds(1, 15)], send_back.at[g], recv_back.at[g, 0]).wait_send()

    def blocks(i, low, high):
        return everything[i // 2, 2 * (i % 2) : 2 * (i % 2) + 2, :, :, low:high].reshape(256, high - low)

    for chip in range(16):
        lanes = slice(chip * LANES, (chip + 1) * LANES)
        parts = everything[chip // 4, chip % 4, 0, 0:16, DIAG:].astype(F32)
        mean = (parts[0:1] + parts[1:2] + parts[2:3]) / sample_total
        inverse = 1.0 / jnp.sqrt(mean + EPSILON)
        scale[0:1, lanes] = inverse
        extra[0:1, lanes] = inverse * mean * inverse - 1.0
        for part in range(2):
            source = slice(GRAM + part * LANES, GRAM + (part + 1) * LANES)
            start[part * 64 : part * 64 + 64, lanes] = everything[chip // 4, chip % 4, core, :, source].astype(F32) * inverse
        start[128:, lanes] = pool[:, lanes].astype(F32) * inverse
    for pair in range(4):
        for side in range(2):
            span = slice(side * LANES, (side + 1) * LANES)
            others = slice((1 - side) * LANES, (2 - side) * LANES)
            corner[pair, span, span] = blocks(pair, GRAM - LANES, GRAM)[span]
            corner[pair, others, span] = blocks(pair + 4, GRAM - LANES, GRAM)[span].astype(F32).T.astype(BF16)
    held[...] = start[...] * (1.0 / 16.0)

    @pl.loop(0, 4)
    def _(turn):
        factor = jnp.where(turn == 0, -0.3125, jnp.where(turn == 1, 0.375, jnp.where(turn == 2, -0.5, 1.0)))
        for j in range(8):
            lanes = slice(j * 256, (j + 1) * 256)
            scaled = (held[:, lanes] * scale[0:1, lanes]).astype(BF16)
            ready[:, lanes] = scaled
            if j < 3:
                ready[:, 2048 + j * 256 : 2048 + (j + 1) * 256] = scaled
        for j in range(8):
            lanes = slice(j * 256, (j + 1) * 256)
            out = lanes_dot(ready[:, (j + 1) * 256 : (j + 4) * 256], blocks(j, 256, 1024))
            for d in range(4):
                i = (j - d) % 8
                out += jnp.dot(
                    ready[:, i * 256 : (i + 1) * 256], blocks(i, d * 256, (d + 1) * 256), preferred_element_type=F32
                )
            if j >= 4:
                out += jnp.dot(ready[:, (j - 4) * 256 : (j - 3) * 256], corner[j - 4], preferred_element_type=F32)
            else:
                out += lanes_dot(ready[:, (j + 4) * 256 : (j + 5) * 256], corner[j])
            held[:, lanes] = (
                out * (scale[0:1, lanes] * (1.0 / sample_total))
                + held[:, lanes] * extra[0:1, lanes]
                + factor * start[:, lanes]
            )

    whitened[...] = held[...].astype(BF16)
    swap = remote(whitened.at[pl.ds(0, 128)], twin_rows, core_send.at[2], core_recv.at[2], twin)
    wide = whitened[128:].astype(F32)
    squares = wide * wide
    ones = jnp.ones((8, LANES), BF16)
    row_norms = jnp.zeros((8, 64), F32)
    for chip in range(16):
        part = squares[:, chip * LANES : (chip + 1) * LANES]
        for _ in range(3):
            piece = part.astype(BF16)
            row_norms += lanes_dot(ones, piece)
            part -= piece.astype(F32)

    def closest(centre_rows):
        wide = centre_rows.astype(F32)
        norms = jnp.sum(wide * wide, axis=1, keepdims=True)
        squared = row_norms[0:1] + norms - 2.0 * lanes_dot(centre_rows, whitened[128:])
        return jnp.min(jnp.maximum(squared, 0.0), axis=0, keepdims=True)

    best = closest(whitened[0:128])
    swap.wait()
    best = jnp.minimum(best, closest(twin_rows[...]))
    nearest[...] = best / (2.0 * 16 * LANES)


VMEM = pl.BlockSpec(memory_space=pltpu.VMEM)
HBM = pl.BlockSpec(memory_space=pltpu.HBM)
DMA = pltpu.SemaphoreType.DMA
LIMIT = 56 * 1024 * 1024


def per_device(sample, pool, old_min, centers):
    width = sample.shape[1]
    sample_total = sample.shape[0] * lax.axis_size("dp") * lax.axis_size("feat")
    nearest = pl.pallas_call(
        lambda *refs: update_kernel(float(sample_total), *refs),
        out_shape=jax.ShapeDtypeStruct((1, pool.shape[0]), F32),
        in_specs=[HBM, HBM, VMEM],
        out_specs=VMEM,
        scratch_shapes=[
            pltpu.VMEM(sample.shape, BF16),
            pltpu.VMEM(pool.shape, BF16),
            pltpu.VMEM((16, 6, 32, LANES), BF16),
            pltpu.VMEM((16, 5, 32, LANES), BF16),
            pltpu.VMEM((6, 512, LANES), BF16),
            pltpu.VMEM((5, 512, LANES), BF16),
            pltpu.VMEM((2, 2, 64, 768), F32),
            pltpu.VMEM((2, 64, 768), F32),
            pltpu.VMEM((2, 64, 768), BF16),
            pltpu.VMEM((2, 16, 8, 384), BF16),
            pltpu.VMEM((2, 8, 384), BF16),
            pltpu.VMEM((4, 4, 2, 64, SLAB), BF16),
            pltpu.VMEM((192, width), F32),
            pltpu.VMEM((192, width), F32),
            pltpu.VMEM((192, width + 768), BF16),
            pltpu.VMEM((4, 256, 256), BF16),
            pltpu.VMEM((8, width), F32),
            pltpu.VMEM((8, width), F32),
            pltpu.VMEM((192, width), BF16),
            pltpu.VMEM((128, width), BF16),
            DMA((8,)),
            DMA((2,)),
            DMA((2,)),
            DMA((3,)),
            DMA((3,)),
            DMA((2,)),
            DMA((2,)),
            DMA((2,)),
            DMA((2, 4)),
            DMA((8, 2)),
            DMA((8, 7)),
        ],
        compiler_params=pltpu.CompilerParams(collective_id=0, has_side_effects=True, vmem_limit_bytes=LIMIT),
    )(sample, pool, centers.reshape(1, 256))
    return jnp.minimum(old_min, nearest.reshape(old_min.shape))


def solution(mesh):
    return jax.shard_map(
        per_device,
        mesh=mesh,
        in_specs=(P(("dp", "feat"), None), P(("dp", "feat"), None), P(("dp", "feat")), P()),
        out_specs=P(("dp", "feat")),
        check_vma=False,
    )
```

time: 99.5 us -> 94.3 us (0.948)
  Pallas kernels: 95.2 us -> 92.2 us
  local copies, waits for them, and re-layouts: 2.54 us -> 0.01 us
    pallas_call x2 -> x1, Pallas kernels: 95.2 us -> 92.2 us  [per_device(): pl.pallas_call(lambda *refs: update_kernel(float(sample_total), *refs), o...]
    unnamed x10 -> x2, local copies, waits for them, and re-layouts: 2.54 us -> 0.01 us
where the time goes in v4:
time: 94.3 us; the launch traced here: 93.3 us
  Pallas kernels  92.2 us (98%)
  other arithmetic  1.11 us (1%)
    pallas_call x1, Pallas kernels, per_device(): pl.pallas_call(lambda *refs: update_kernel(float(sample_total), *refs), o...  92.2 us

profile of v4, /device:TPU:1, one launch (start us, length us, event | category | flops | bytes accessed | tf_op | source)
XLA Modules:
  0.0 93.3 jit_solution(8414603856187739001)
XLA Ops:
  0.0 0.0 copy-start
  0.0 92.2 %shard_map.46 = f32[1,64]{1,0:T(1,128)} custom-call(bf16[32,2048]{1,0:T(8,128)(2,1)} %refs_0_.1, bf16[64,2048]{1,0:T(8,128)(2,1)} %refs_1_.1, s32[1,256]{1,0:T(1,128)} %bitcast.3), custom_call_target="tpu_custom_call" | custom-call | tf_op jit(solution)/shard_map/pallas_call | solution.py:356
  92.2 0.0 copy-done
  92.2 1.1 %bitcast_minimum_fusion = f32[64]{0:T(128)} fusion(f32[64]{0:T(128)S(1)} %copy-done, f32[1,64]{1,0:T(1,128)} %shard_map.46), kind=kLoop, calls=%fused_computation | loop fusion | flops 64 | bytes 768 | tf_op jit(solution)/shard_map/min | solution.py:396
Async XLA Ops:
  0.0 92.2 %copy-start = (f32[64]{0:T(128)S(1)}, f32[64]{0:T(128)}, u32[]{:S(2)}) copy-start(f32[64]{0:T(128)} %param.6) | copy-start | bytes 772

commit v5 on v4

--- a/solution.py
+++ b/solution.py
@@ -131,7 +131,7 @@
         return ref.at[pl.ds(pl.multiple_of((k // 2) * 8, 8), 8), pl.ds(pl.multiple_of((k % 2) * 384, 384), 384)]
 
     def slab(g):
-        return everything.at[x, y, core, :, pl.ds(g * 768, 768)]
+        return everything.at[x // 2, x % 2, y // 2, y % 2, core, :, pl.ds(g * 768, 768)]
 
     def reduce_begin(g):
         remote(partial.at[g, 1 - core], other.at[g], core_send.at[g], core_recv.at[g], twin).wait()
@@ -177,26 +177,32 @@
             self.q = [(q + 4 - d) % 4 for d in range(4)]
             number = group * 4 + shift
             self.sent = [strip_send.at[number, n] for n in range(2)]
-            self.got = [strip_recv.at[number, n] for n in range(7)]
+            self.got = [strip_recv.at[number, n] for n in range(9)]
 
         def where(self, p, q):
             return device(q, p, z, core) if self.flip else device(p, q, z, core)
 
+        def at(self, p, q):
+            first, second = (q, p) if self.flip else (p, q)
+            return everything.at[first + second + (core,) + self.place]
+
         def piece(self, p, q):
-            return everything.at[(q, p, core) + self.place] if self.flip else everything.at[(p, q, core) + self.place]
-
-        def line(self, q, side=None):
-            every, side = slice(None), core if side is None else side
-            return everything.at[(q, every, side) + self.place] if self.flip else everything.at[(every, q, side) + self.place]
+            return self.at((p // 2, p % 2), (q // 2, q % 2))
+
+        def pair(self, parity, q):
+            return self.at((slice(None), parity), (q // 2, q % 2))
+
+        def line(self, q):
+            return self.at((slice(None), slice(None)), (q // 2, q % 2))
 
         def across(self, n):
             piece = self.piece(self.p[n], self.q[0])
-            for d in (2, 1, 3):
-                remote(piece, piece, self.sent[0], self.got[3 + d - 1], self.where(self.p[0], self.q[4 - d]))
+            remote(piece, piece, self.sent[0], self.got[3 + n % 2], self.where(self.p[0], self.q[3]))
+            remote(piece, piece, self.sent[0], self.got[5 + n % 2], self.where(self.p[0], self.q[1]))
 
         def twins(self, d):
             line = self.line(self.q[d])
-            remote(line, line, self.sent[1], self.got[6], twin)
+            remote(line, line, self.sent[1], self.got[8], twin)
 
         def begin(self):
             if self.shift == 0:
@@ -215,14 +221,26 @@
                 self.across(d)
             self.twins(0)
 
+        def forward(self):
+            same, other = self.p[0] % 2, 1 - self.p[0] % 2
+            up, down = self.pair(same, self.q[1]), self.pair(other, self.q[3])
+            bytes_of(up, self.sent[0], self.got[3]).wait_recv()
+            remote(up, up, self.sent[0], self.got[7], self.where(self.p[0], self.q[3]))
+            bytes_of(down, self.sent[0], self.got[6]).wait_recv()
+            remote(down, down, self.sent[0], self.got[7], self.where(self.p[0], self.q[1]))
+            bytes_of(self.pair(other, self.q[1]), self.sent[0], self.got[4]).wait_recv()
+            self.twins(1)
+            bytes_of(self.pair(same, self.q[3]), self.sent[0], self.got[5]).wait_recv()
+            self.twins(3)
+
         def finish(self):
-            for d in (1, 3, 2):
-                bytes_of(self.line(self.q[d]), self.sent[0], self.got[3 + d - 1]).wait_recv()
-                self.twins(d)
+            bytes_of(self.line(self.q[2]), self.sent[0], self.got[7]).wait_recv()
+            self.twins(2)
 
         def last(self):
-            whole = everything.at[(slice(None), slice(None), 1 - core) + self.place]
-            bytes_of(whole, self.sent[1], self.got[6]).wait()
+            every = slice(None)
+            whole = everything.at[(every, every, every, every, 1 - core) + self.place]
+            bytes_of(whole, self.sent[1], self.got[8]).wait()
             bytes_of(landed_a.at[pl.ds(0, 3), pl.ds(0, 480), :], self.sent[0], self.got[0]).wait_send()
 
     first = exchange(0)
@@ -259,30 +277,33 @@
     a0, a1, a2, a3 = [Strip(0, shift, shift % 2 == 1) for shift in (0, 1, 3, 2)]
     b0, b1, b2, b3 = [Strip(1, shift, shift % 2 == 1) for shift in (0, 1, 3, 2)]
     a0.begin()
-    a0.middle()
     reduce_end(1)
     a1.begin(), a2.begin(), a3.begin()
-    a1.middle(), a2.middle(), b0.begin(), a3.middle(), a0.finish(), b0.middle()
-    b1.begin(), b2.begin(), a1.finish(), a2.finish(), b3.begin(), b1.middle(), b2.middle(), b3.middle()
-    a3.finish(), b0.finish(), b1.finish(), b2.finish(), b3.finish()
+    a0.middle(), a1.middle(), a2.middle(), b0.begin(), a3.middle()
+    b1.begin(), b2.begin(), b3.begin()
+    a0.forward(), a1.forward(), a2.forward(), a3.forward()
+    b0.middle(), b1.middle(), b2.middle(), b3.middle()
+    a0.finish(), a1.finish(), a2.finish(), a3.finish()
+    b0.forward(), b1.forward(), b2.forward(), b3.forward()
+    b0.finish(), b1.finish(), b2.finish(), b3.finish()
     for strip in (a0, a1, a2, a3, b0, b1, b2, b3):
         strip.last()
     for g in range(2):
         bytes_of(terms.at[g, pl.ds(1, 15)], send_back.at[g], recv_back.at[g, 0]).wait_send()
 
     def blocks(i, low, high):
-        return everything[i // 2, 2 * (i % 2) : 2 * (i % 2) + 2, :, :, low:high].reshape(256, high - low)
+        return everything[i // 4, (i // 2) % 2, i % 2, :, :, :, low:high].reshape(256, high - low)
 
     for chip in range(16):
         lanes = slice(chip * LANES, (chip + 1) * LANES)
-        parts = everything[chip // 4, chip % 4, 0, 0:16, DIAG:].astype(F32)
+        parts = everything[chip // 8, (chip // 4) % 2, (chip // 2) % 2, chip % 2, 0, 0:16, DIAG:].astype(F32)
         mean = (parts[0:1] + parts[1:2] + parts[2:3]) / sample_total
         inverse = 1.0 / jnp.sqrt(mean + EPSILON)
         scale[0:1, lanes] = inverse
         extra[0:1, lanes] = inverse * mean * inverse - 1.0
         for part in range(2):
             source = slice(GRAM + part * LANES, GRAM + (part + 1) * LANES)
-            start[part * 64 : part * 64 + 64, lanes] = everything[chip // 4, chip % 4, core, :, source].astype(F32) * inverse
+            start[part * 64 : part * 64 + 64, lanes] = everything[chip // 8, (chip // 4) % 2, (chip // 2) % 2, chip % 2, core, :, source].astype(F32) * inverse
         start[128:, lanes] = pool[:, lanes].astype(F32) * inverse
     for pair in range(4):
         for side in range(2):
@@ -370,7 +391,7 @@
             pltpu.VMEM((2, 64, 768), BF16),
             pltpu.VMEM((2, 16, 8, 384), BF16),
             pltpu.VMEM((2, 8, 384), BF16),
-            pltpu.VMEM((4, 4, 2, 64, SLAB), BF16),
+            pltpu.VMEM((2, 2, 2, 2, 2, 64, SLAB), BF16),
             pltpu.VMEM((192, width), F32),
             pltpu.VMEM((192, width), F32),
             pltpu.VMEM((192, width + 768), BF16),
@@ -389,7 +410,7 @@
             DMA((2,)),
             DMA((2, 4)),
             DMA((8, 2)),
-            DMA((8, 7)),
+            DMA((8, 9)),
         ],
         compiler_params=pltpu.CompilerParams(collective_id=0, has_side_effects=True, vmem_limit_bytes=LIMIT),
     )(sample, pool, centers.reshape(1, 256))

time: 94.3 us -> 87.7 us (0.930)
  Pallas kernels: 92.2 us -> 86.4 us
    pallas_call x1, Pallas kernels: 92.2 us -> 86.4 us  [per_device(): pl.pallas_call(lambda *refs: update_kernel(float(sample_total), *refs), o...]
where the time goes in v5:
time: 87.7 us; the launch traced here: 87.6 us
  Pallas kernels  86.4 us (99%)
  other arithmetic  1.11 us (1%)
    pallas_call x1, Pallas kernels, per_device(): pl.pallas_call(lambda *refs: update_kernel(float(sample_total), *refs), o...  86.4 us

profile of v5, /device:TPU:1, one launch (start us, length us, event | category | flops | bytes accessed | tf_op | source)
XLA Modules:
  0.0 87.6 jit_solution(16461208628332338431)
XLA Ops:
  0.0 0.0 copy-start
  0.0 86.4 %shard_map.46 = f32[1,64]{1,0:T(1,128)} custom-call(bf16[32,2048]{1,0:T(8,128)(2,1)} %refs_0_.1, bf16[64,2048]{1,0:T(8,128)(2,1)} %refs_1_.1, s32[1,256]{1,0:T(1,128)} %bitcast.3), custom_call_target="tpu_custom_call" | custom-call | tf_op jit(solution)/shard_map/pallas_call | solution.py:377
  86.4 0.0 copy-done
  86.4 1.1 %bitcast_minimum_fusion = f32[64]{0:T(128)} fusion(f32[64]{0:T(128)S(1)} %copy-done, f32[1,64]{1,0:T(1,128)} %shard_map.46), kind=kLoop, calls=%fused_computation | loop fusion | flops 64 | bytes 768 | tf_op jit(solution)/shard_map/min | solution.py:417
Async XLA Ops:
  0.0 86.4 %copy-start = (f32[64]{0:T(128)S(1)}, f32[64]{0:T(128)}, u32[]{:S(2)}) copy-start(f32[64]{0:T(128)} %param.6) | copy-start | bytes 772

commit v6 on v5

--- a/solution.py
+++ b/solution.py
@@ -12,8 +12,10 @@
 LANES = 128
 PANELS = 9
 SLAB = 1536
-GRAM = PANELS * LANES
-DIAG = SLAB - LANES
+GRAM = LANES
+CENTRE = GRAM + PANELS * LANES
+GROUPS = ((0, 768), (768, 512), (1280, 256))
+PARTS = ((0, 5), (5, 4), (9, 2))
 
 
 def position():
@@ -59,8 +61,8 @@
 
 
 def update_kernel(
-    sample_total, sample_in, pool_in, centers, nearest, sample, pool, parcels_a, parcels_b, landed_a, landed_b, partial, other, mine,
-    terms, chunk, everything, start, held, ready, corner, scale, extra, whitened, twin_rows, local, plane_send, plane_recv,
+    sample_total, sample_in, pool_in, centers, nearest, sample, pool, parcels, landed, partial, other, mine,
+    terms_a, terms_b, terms_c, chunk_a, chunk_b, chunk_c, everything, start, held, ready, corner, scale, extra, whitened, twin_rows, local, plane_send, plane_recv,
     core_send, core_recv, send, recv, send_back, recv_back, strip_send, strip_recv,
 ):
     x, y, z, core = position()
@@ -85,13 +87,9 @@
         copy.wait()
     for chip in range(16):
         for step, panel in enumerate(column_panels(chip)):
-            block = sample[:, panel * LANES : (panel + 1) * LANES]
-            if step < 6:
-                parcels_a[chip, step] = block
-            else:
-                parcels_b[chip, step - 6] = block
+            parcels[chip, step] = sample[:, panel * LANES : (panel + 1) * LANES]
         for part in range(2):
-            parcels_b[chip, 3 + part] = pool[part * 32 : part * 32 + 32, chip * LANES : (chip + 1) * LANES]
+            parcels[chip, PANELS + part] = pool[part * 32 : part * 32 + 32, chip * LANES : (chip + 1) * LANES]
     pl.semaphore_wait(barrier, len(partners))
 
     def bytes_of(ref, send_sem, recv_sem):
@@ -100,69 +98,80 @@
         )
 
     rows = pl.ds(pl.multiple_of(here * 32, 32), 32)
-    parcels, landed = [parcels_a, parcels_b], [landed_a, landed_b]
+    terms, chunk = [terms_a, terms_b, terms_c], [chunk_a, chunk_b, chunk_c]
 
     def exchange(g):
+        panels = pl.ds(*PARTS[g])
         for dx, dy in offsets:
             to_x, to_y = (x + dx) % 4, (y + dy) % 4
             remote(
-                parcels[g].at[to_x * 4 + to_y],
-                landed[g].at[:, rows, :],
+                parcels.at[to_x * 4 + to_y, panels],
+                landed.at[panels, rows, :],
                 plane_send.at[g],
                 plane_recv.at[g],
                 device(to_x, to_y, z, core),
             )
-        own = pltpu.make_async_copy(parcels[g].at[here], landed[g].at[:, rows, :], local.at[2 + g])
+        own = pltpu.make_async_copy(parcels.at[here, panels], landed.at[panels, rows, :], local.at[2 + g])
         own.start()
         own.wait()
-        return bytes_of(landed[g].at[:, pl.ds(0, 480), :], plane_send.at[g], plane_recv.at[g])
+        return bytes_of(landed.at[panels, pl.ds(0, 480), :], plane_send.at[g], plane_recv.at[g])
 
     half = y % 2
 
-    def block_of(step):
-        block = rows_dot(landed_a[half], landed_a[step] if step < 6 else landed_b[step - 6])
-        if step < 2:
-            down = lax.broadcasted_iota(jnp.int32, block.shape, 0)
-            along = lax.broadcasted_iota(jnp.int32, block.shape, 1)
-            block = jnp.where((down == along) & (half == step), 0.0, block)
-        return block
-
-    def tiles(ref, k):
-        return ref.at[pl.ds(pl.multiple_of((k // 2) * 8, 8), 8), pl.ds(pl.multiple_of((k % 2) * 384, 384), 384)]
-
-    def slab(g):
-        return everything.at[x // 2, x % 2, y // 2, y % 2, core, :, pl.ds(g * 768, 768)]
+    def fill_moments(first, count):
+        for step in range(first, first + count):
+            block = rows_dot(landed[half], landed[step])
+            if step < 2:
+                down = lax.broadcasted_iota(jnp.int32, block.shape, 0)
+                along = lax.broadcasted_iota(jnp.int32, block.shape, 1)
+                block = jnp.where((down == along) & (half == step), 0.0, block)
+            lanes = slice(GRAM + step * LANES, GRAM + (step + 1) * LANES)
+            partial[0, :, lanes] = block[:64]
+            partial[1, :, lanes] = block[64:]
+
+    def tiles(ref, k, width):
+        return ref.at[pl.ds(pl.multiple_of((k // 2) * 8, 8), 8), pl.ds(pl.multiple_of((k % 2) * width, width), width)]
+
+    def group(ref, g):
+        return ref.at[:, pl.ds(*GROUPS[g])]
 
     def reduce_begin(g):
-        remote(partial.at[g, 1 - core], other.at[g], core_send.at[g], core_recv.at[g], twin).wait()
+        low, wide = GROUPS[g]
+        lanes = pl.ds(low, wide)
+        remote(partial.at[1 - core, :, lanes], other.at[:, lanes], core_send.at[g], core_recv.at[g], twin).wait()
         if g == 0:
-            mine[g] = (partial[g, core] + other[g]).astype(BF16)
+            mine[:, LANES:wide] = (partial[core, :, LANES:wide] + other[:, LANES:wide]).astype(BF16)
+            squares = partial[core, 0:1, :LANES] + other[0:1, :LANES]
+            mine[0:16, :LANES] = in_three(squares, 16).astype(BF16)
+            mine[16:64, :LANES] = jnp.zeros((48, LANES), BF16)
         else:
-            mine[g, :, :640] = (partial[g, core, :, :640] + other[g, :, :640]).astype(BF16)
-            squares = partial[g, core, 0:1, 640:] + other[g, 0:1, 640:]
-            mine[g, 0:16, 640:] = in_three(squares, 16).astype(BF16)
-            mine[g, 16:64, 640:] = jnp.zeros((48, LANES), BF16)
-        own = pltpu.make_async_copy(tiles(mine.at[g], z), terms.at[g, 0], local.at[4 + g])
+            mine[:, lanes] = (partial[core, :, lanes] + other[:, lanes]).astype(BF16)
+        own = pltpu.make_async_copy(tiles(group(mine, g), z, wide // 2), terms[g].at[0], local.at[5 + g])
         own.start()
         for o in far_first:
-            remote(tiles(mine.at[g], column[o]), terms.at[g, o], send.at[g], recv.at[g], device(x, y, column[o], core))
+            remote(
+                tiles(group(mine, g), column[o], wide // 2), terms[g].at[o], send.at[g], recv.at[g], device(x, y, column[o], core)
+            )
         own.wait()
 
     def reduce_end(g):
-        bytes_of(terms.at[g, pl.ds(1, 15)], send.at[g], recv.at[g]).wait()
-        total = terms[g, 0].astype(F32)
+        width = GROUPS[g][1] // 2
+        bytes_of(terms[g].at[pl.ds(1, 15)], send.at[g], recv.at[g]).wait()
+        total = terms[g][0].astype(F32)
         for o in range(1, 16):
-            total += terms[g, o].astype(F32)
+            total += terms[g][o].astype(F32)
         if g == 0:
-            chunk[g] = total.astype(BF16)
+            squares = total[0:1, :LANES] + total[1:2, :LANES] + total[2:3, :LANES]
+            chunk[g][:, :LANES] = jnp.where(z == 0, in_three(squares, 8), total[:, :LANES]).astype(BF16)
+            chunk[g][:, LANES:] = total[:, LANES:].astype(BF16)
         else:
-            squares = total[0:1, 256:] + total[1:2, 256:] + total[2:3, 256:]
-            chunk[g, :, :256] = total[:, :256].astype(BF16)
-            chunk[g, :, 256:] = jnp.where(z == 1, in_three(squares, 8), total[:, 256:]).astype(BF16)
-        own = pltpu.make_async_copy(chunk.at[g], tiles(slab(g), z), local.at[6 + g])
+            chunk[g][...] = total.astype(BF16)
+        place = tiles(group(everything.at[x // 2, x % 2, y // 2, y % 2, core], g), z, width)
+        own = pltpu.make_async_copy(chunk[g], place, local.at[8 + g])
         own.start()
+        zone_of = z // 4 if g == 0 else 0
         for o in far_first:
-            remote(chunk.at[g], tiles(slab(g), z), send_back.at[g], recv_back.at[g, z // 4], device(x, y, column[o], core))
+            remote(chunk[g], place, send_back.at[g], recv_back.at[g, zone_of], device(x, y, column[o], core))
         own.wait()
 
     zone = z // 4
@@ -170,12 +179,13 @@
     class Strip:
         def __init__(self, group, shift, flip):
             self.group, self.shift, self.flip = group, shift, flip
-            self.a = (zone + shift) % 4
-            self.place = (pl.ds(pl.multiple_of(self.a * 16, 16), 16), pl.ds(group * 768, 768))
+            count = 16 if group == 0 else 32
+            self.a = (zone + shift) % 4 if group == 0 else shift
+            self.place = (pl.ds(pl.multiple_of(self.a * count, count), count), pl.ds(*GROUPS[group]))
             p, q = (y, x) if flip else (x, y)
             self.p = [(p + 4 - d) % 4 for d in range(4)]
             self.q = [(q + 4 - d) % 4 for d in range(4)]
-            number = group * 4 + shift
+            number = (0, 4, 6)[group] + shift
             self.sent = [strip_send.at[number, n] for n in range(2)]
             self.got = [strip_recv.at[number, n] for n in range(9)]
 
@@ -205,11 +215,11 @@
             remote(line, line, self.sent[1], self.got[8], twin)
 
         def begin(self):
-            if self.shift == 0:
-                ref = terms.at[self.group, pl.ds(0, 3)]
-            else:
-                ref = self.piece(self.p[0], self.q[0])
-            bytes_of(ref, send_back.at[self.group], recv_back.at[self.group, self.a]).wait_recv()
+            if self.group == 0:
+                ref = terms_a.at[pl.ds(0, 3)] if self.shift == 0 else self.piece(self.p[0], self.q[0])
+                bytes_of(ref, send_back.at[0], recv_back.at[0, self.a]).wait_recv()
+            elif self.shift == 0:
+                bytes_of(terms[self.group].at[pl.ds(1, 15)], send_back.at[self.group], recv_back.at[self.group, 0]).wait_recv()
             piece = self.piece(self.p[0], self.q[0])
             for d in (2, 1, 3):
                 remote(piece, piece, self.sent[0], self.got[d - 1], self.where(self.p[4 - d], self.q[0]))
@@ -241,7 +251,7 @@
             every = slice(None)
             whole = everything.at[(every, every, every, every, 1 - core) + self.place]
             bytes_of(whole, self.sent[1], self.got[8]).wait()
-            bytes_of(landed_a.at[pl.ds(0, 3), pl.ds(0, 480), :], self.sent[0], self.got[0]).wait_send()
+            bytes_of(landed.at[pl.ds(0, (3, 4, 2)[self.group]), pl.ds(0, 480), :], self.sent[0], self.got[0]).wait_send()
 
     first = exchange(0)
     row = lax.broadcasted_iota(jnp.int32, (512, 256), 0)
@@ -251,66 +261,72 @@
     first.wait_send()
     second = exchange(1)
     first.wait_recv()
-    for step in range(6):
-        block = block_of(step)
-        lanes = slice(step * LANES, (step + 1) * LANES)
-        partial[0, 0, :, lanes] = block[:64]
-        partial[0, 1, :, lanes] = block[64:]
-    reduce_begin(0)
-    wide = landed_a[half].astype(F32)
+    fill_moments(*PARTS[0])
+    wide = landed[half].astype(F32)
     squares = jnp.sum(wide * wide, axis=0, keepdims=True)
     top = lax.broadcasted_iota(jnp.int32, (64, LANES), 0) == 0
     for side in range(2):
-        partial[1, side, :, 640:] = jnp.where(top, squares, 0.0)
-    second.wait()
-    for step in range(6, PANELS):
-        block = block_of(step)
-        lanes = slice((step - 6) * LANES, (step - 5) * LANES)
-        partial[1, 0, :, lanes] = block[:64]
-        partial[1, 1, :, lanes] = block[64:]
-    picked = rows_dot(chosen[0], landed_b[3]) + rows_dot(chosen[1], landed_b[4])
+        partial[side, :, :LANES] = jnp.where(top, squares, 0.0)
+    reduce_begin(0)
+    second.wait_send()
+    third = exchange(2)
+    second.wait_recv()
+    fill_moments(*PARTS[1])
+    reduce_begin(1)
+    third.wait()
+    picked = rows_dot(chosen[0], landed[PANELS]) + rows_dot(chosen[1], landed[PANELS + 1])
     for part in range(4):
-        lanes = slice(384 + (part % 2) * LANES, 384 + (part % 2 + 1) * LANES)
-        partial[1, part // 2, :, lanes] = picked[part * 64 : part * 64 + 64]
-    reduce_begin(1)
+        lanes = slice(CENTRE + (part % 2) * LANES, CENTRE + (part % 2 + 1) * LANES)
+        partial[part // 2, :, lanes] = picked[part * 64 : part * 64 + 64]
+    reduce_begin(2)
     reduce_end(0)
-    a0, a1, a2, a3 = [Strip(0, shift, shift % 2 == 1) for shift in (0, 1, 3, 2)]
-    b0, b1, b2, b3 = [Strip(1, shift, shift % 2 == 1) for shift in (0, 1, 3, 2)]
-    a0.begin()
+    strips_a = [Strip(0, shift, shift % 2 == 1) for shift in (0, 1, 3, 2)]
+    strips_b = [Strip(1, shift, shift == 1) for shift in (0, 1)]
+    strips_c = [Strip(2, shift, shift == 1) for shift in (0, 1)]
+
+    def every(strips, what):
+        for strip in strips:
+            getattr(strip, what)()
+
+    strips_a[0].begin()
     reduce_end(1)
-    a1.begin(), a2.begin(), a3.begin()
-    a0.middle(), a1.middle(), a2.middle(), b0.begin(), a3.middle()
-    b1.begin(), b2.begin(), b3.begin()
-    a0.forward(), a1.forward(), a2.forward(), a3.forward()
-    b0.middle(), b1.middle(), b2.middle(), b3.middle()
-    a0.finish(), a1.finish(), a2.finish(), a3.finish()
-    b0.forward(), b1.forward(), b2.forward(), b3.forward()
-    b0.finish(), b1.finish(), b2.finish(), b3.finish()
-    for strip in (a0, a1, a2, a3, b0, b1, b2, b3):
-        strip.last()
-    for g in range(2):
-        bytes_of(terms.at[g, pl.ds(1, 15)], send_back.at[g], recv_back.at[g, 0]).wait_send()
+    every(strips_a[1:], "begin")
+    reduce_end(2)
+    every(strips_a, "middle")
+    every(strips_b, "begin")
+    every(strips_a, "forward")
+    every(strips_c, "begin")
+    every(strips_b, "middle")
+    every(strips_a, "finish")
+    every(strips_c, "middle")
+    every(strips_b, "forward")
+    every(strips_c, "forward")
+    every(strips_b, "finish")
+    every(strips_c, "finish")
+    every(strips_a + strips_b + strips_c, "last")
+    for g in range(3):
+        bytes_of(terms[g].at[pl.ds(1, 15)], send_back.at[g], recv_back.at[g, 0]).wait_send()
 
     def blocks(i, low, high):
         return everything[i // 4, (i // 2) % 2, i % 2, :, :, :, low:high].reshape(256, high - low)
 
     for chip in range(16):
         lanes = slice(chip * LANES, (chip + 1) * LANES)
-        parts = everything[chip // 8, (chip // 4) % 2, (chip // 2) % 2, chip % 2, 0, 0:16, DIAG:].astype(F32)
+        parts = everything[chip // 8, (chip // 4) % 2, (chip // 2) % 2, chip % 2, 0, 0:16, :LANES].astype(F32)
         mean = (parts[0:1] + parts[1:2] + parts[2:3]) / sample_total
         inverse = 1.0 / jnp.sqrt(mean + EPSILON)
         scale[0:1, lanes] = inverse
         extra[0:1, lanes] = inverse * mean * inverse - 1.0
         for part in range(2):
-            source = slice(GRAM + part * LANES, GRAM + (part + 1) * LANES)
+            source = slice(CENTRE + part * LANES, CENTRE + (part + 1) * LANES)
             start[part * 64 : part * 64 + 64, lanes] = everything[chip // 8, (chip // 4) % 2, (chip // 2) % 2, chip % 2, core, :, source].astype(F32) * inverse
         start[128:, lanes] = pool[:, lanes].astype(F32) * inverse
     for pair in range(4):
         for side in range(2):
             span = slice(side * LANES, (side + 1) * LANES)
             others = slice((1 - side) * LANES, (2 - side) * LANES)
-            corner[pair, span, span] = blocks(pair, GRAM - LANES, GRAM)[span]
-            corner[pair, others, span] = blocks(pair + 4, GRAM - LANES, GRAM)[span].astype(F32).T.astype(BF16)
+            corner[pair, span, span] = blocks(pair, CENTRE - LANES, CENTRE)[span]
+            corner[pair, others, span] = blocks(pair + 4, CENTRE - LANES, CENTRE)[span].astype(F32).T.astype(BF16)
     held[...] = start[...] * (1.0 / 16.0)
 
     @pl.loop(0, 4)
@@ -324,11 +340,11 @@
                 ready[:, 2048 + j * 256 : 2048 + (j + 1) * 256] = scaled
         for j in range(8):
             lanes = slice(j * 256, (j + 1) * 256)
-            out = lanes_dot(ready[:, (j + 1) * 256 : (j + 4) * 256], blocks(j, 256, 1024))
+            out = lanes_dot(ready[:, (j + 1) * 256 : (j + 4) * 256], blocks(j, GRAM + 256, GRAM + 1024))
             for d in range(4):
                 i = (j - d) % 8
                 out += jnp.dot(
-                    ready[:, i * 256 : (i + 1) * 256], blocks(i, d * 256, (d + 1) * 256), preferred_element_type=F32
+                    ready[:, i * 256 : (i + 1) * 256], blocks(i, GRAM + d * 256, GRAM + (d + 1) * 256), preferred_element_type=F32
                 )
             if j >= 4:
                 out += jnp.dot(ready[:, (j - 4) * 256 : (j - 3) * 256], corner[j - 4], preferred_element_type=F32)
@@ -341,7 +357,7 @@
             )
 
     whitened[...] = held[...].astype(BF16)
-    swap = remote(whitened.at[pl.ds(0, 128)], twin_rows, core_send.at[2], core_recv.at[2], twin)
+    swap = remote(whitened.at[pl.ds(0, 128)], twin_rows, core_send.at[3], core_recv.at[3], twin)
     wide = whitened[128:].astype(F32)
     squares = wide * wide
     ones = jnp.ones((8, LANES), BF16)
@@ -382,15 +398,13 @@
         scratch_shapes=[
             pltpu.VMEM(sample.shape, BF16),
             pltpu.VMEM(pool.shape, BF16),
-            pltpu.VMEM((16, 6, 32, LANES), BF16),
-            pltpu.VMEM((16, 5, 32, LANES), BF16),
-            pltpu.VMEM((6, 512, LANES), BF16),
-            pltpu.VMEM((5, 512, LANES), BF16),
-            pltpu.VMEM((2, 2, 64, 768), F32),
-            pltpu.VMEM((2, 64, 768), F32),
-            pltpu.VMEM((2, 64, 768), BF16),
-            pltpu.VMEM((2, 16, 8, 384), BF16),
-            pltpu.VMEM((2, 8, 384), BF16),
+            pltpu.VMEM((16, PANELS + 2, 32, LANES), BF16),
+            pltpu.VMEM((PANELS + 2, 512, LANES), BF16),
+            pltpu.VMEM((2, 64, SLAB), F32),
+            pltpu.VMEM((64, SLAB), F32),
+            pltpu.VMEM((64, SLAB), BF16),
+            *[pltpu.VMEM((16, 8, wide // 2), BF16) for _, wide in GROUPS],
+            *[pltpu.VMEM((8, wide // 2), BF16) for _, wide in GROUPS],
             pltpu.VMEM((2, 2, 2, 2, 2, 64, SLAB), BF16),
             pltpu.VMEM((192, width), F32),
             pltpu.VMEM((192, width), F32),
@@ -400,15 +414,15 @@
             pltpu.VMEM((8, width), F32),
             pltpu.VMEM((192, width), BF16),
             pltpu.VMEM((128, width), BF16),
-            DMA((8,)),
-            DMA((2,)),
-            DMA((2,)),
+            DMA((11,)),
             DMA((3,)),
             DMA((3,)),
-            DMA((2,)),
-            DMA((2,)),
-            DMA((2,)),
-            DMA((2, 4)),
+            DMA((4,)),
+            DMA((4,)),
+            DMA((3,)),
+            DMA((3,)),
+            DMA((3,)),
+            DMA((3, 4)),
             DMA((8, 2)),
             DMA((8, 9)),
         ],

time: 87.7 us -> 85.7 us (0.977)
  Pallas kernels: 86.4 us -> 84.4 us
    pallas_call x1, Pallas kernels: 86.4 us -> 84.4 us  [per_device(): pl.pallas_call(lambda *refs: update_kernel(float(sample_total), *refs), o...]
where the time goes in v6:
time: 85.7 us; the launch traced here: 85.6 us
  Pallas kernels  84.4 us (98%)
  other arithmetic  1.11 us (1%)
    pallas_call x1, Pallas kernels, per_device(): pl.pallas_call(lambda *refs: update_kernel(float(sample_total), *refs), o...  84.4 us

profile of v6, /device:TPU:1, one launch (start us, length us, event | category | flops | bytes accessed | tf_op | source)
XLA Modules:
  0.0 85.6 jit_solution(10974646313104936753)
XLA Ops:
  0.0 0.0 copy-start
  0.0 84.4 %shard_map.46 = f32[1,64]{1,0:T(1,128)} custom-call(bf16[32,2048]{1,0:T(8,128)(2,1)} %refs_0_.1, bf16[64,2048]{1,0:T(8,128)(2,1)} %refs_1_.1, s32[1,256]{1,0:T(1,128)} %bitcast.3), custom_call_target="tpu_custom_call" | custom-call | tf_op jit(solution)/shard_map/pallas_call | solution.py:393
  84.5 0.0 copy-done
  84.5 1.1 %bitcast_minimum_fusion = f32[64]{0:T(128)} fusion(f32[64]{0:T(128)S(1)} %copy-done, f32[1,64]{1,0:T(1,128)} %shard_map.46), kind=kLoop, calls=%fused_computation | loop fusion | flops 64 | bytes 768 | tf_op jit(solution)/shard_map/min | solution.py:431
Async XLA Ops:
  0.0 84.5 %copy-start = (f32[64]{0:T(128)S(1)}, f32[64]{0:T(128)}, u32[]{:S(2)}) copy-start(f32[64]{0:T(128)} %param.6) | copy-start | bytes 772

commit v7 on v6

--- a/solution.py
+++ b/solution.py
@@ -253,14 +253,12 @@
             bytes_of(whole, self.sent[1], self.got[8]).wait()
             bytes_of(landed.at[pl.ds(0, (3, 4, 2)[self.group]), pl.ds(0, 480), :], self.sent[0], self.got[0]).wait_send()
 
-    first = exchange(0)
+    first, second, third = exchange(0), exchange(1), exchange(2)
     row = lax.broadcasted_iota(jnp.int32, (512, 256), 0)
     owner = ((z // 4) * 4 + ((row >> 5) & 3)) * 32 + (row >> 7) * 8 + (z % 4) * 2 + core
     row_id = owner * 64 + (row & 31)
     chosen = [jnp.where(row_id + part * 32 == centers[...], 1.0, 0.0).astype(BF16) for part in range(2)]
-    first.wait_send()
-    second = exchange(1)
-    first.wait_recv()
+    first.wait()
     fill_moments(*PARTS[0])
     wide = landed[half].astype(F32)
     squares = jnp.sum(wide * wide, axis=0, keepdims=True)
@@ -268,9 +266,7 @@
     for side in range(2):
         partial[side, :, :LANES] = jnp.where(top, squares, 0.0)
     reduce_begin(0)
-    second.wait_send()
-    third = exchange(2)
-    second.wait_recv()
+    second.wait()
     fill_moments(*PARTS[1])
     reduce_begin(1)
     third.wait()

time: 85.7 us -> 86.3 us (level)
  no operation moved by 1% of the time
where the time goes in v7:
time: 86.3 us; the launch traced here: 86.2 us
  Pallas kernels  85 us (98%)
  other arithmetic  1.11 us (1%)
    pallas_call x1, Pallas kernels, per_device(): pl.pallas_call(lambda *refs: update_kernel(float(sample_total), *refs), o...  85 us

profile of v7, /device:TPU:1, one launch (start us, length us, event | category | flops | bytes accessed | tf_op | source)
XLA Modules:
  0.0 86.2 jit_solution(15464605115981901426)
XLA Ops:
  0.0 0.0 copy-start
  0.0 85.0 %shard_map.46 = f32[1,64]{1,0:T(1,128)} custom-call(bf16[32,2048]{1,0:T(8,128)(2,1)} %refs_0_.1, bf16[64,2048]{1,0:T(8,128)(2,1)} %refs_1_.1, s32[1,256]{1,0:T(1,128)} %bitcast.3), custom_call_target="tpu_custom_call" | custom-call | tf_op jit(solution)/shard_map/pallas_call | solution.py:389
  85.0 0.0 copy-done
  85.0 1.1 %bitcast_minimum_fusion = f32[64]{0:T(128)} fusion(f32[64]{0:T(128)S(1)} %copy-done, f32[1,64]{1,0:T(1,128)} %shard_map.46), kind=kLoop, calls=%fused_computation | loop fusion | flops 64 | bytes 768 | tf_op jit(solution)/shard_map/min | solution.py:427
Async XLA Ops:
  0.0 85.0 %copy-start = (f32[64]{0:T(128)S(1)}, f32[64]{0:T(128)}, u32[]{:S(2)}) copy-start(f32[64]{0:T(128)} %param.6) | copy-start | bytes 772
